TPU v7x, 32 devices: a whole 2x2x4 slice. The times are simulated.
32 devices in a mesh: wide: 8 (over z, y), narrow: 4 (over x, core).
Axes of the slice: x: 2, y: 2, z: 4, core: 2. Of those that a mesh axis runs over, the one named last changes fastest.
Arguments:
- patches: bfloat16 [128, 256, 768], P(('wide', 'narrow')), may hold values from -6 to 6
- counts: int32 [128], P(('wide', 'narrow')), may hold values from 16 to 256, as said below
- cotangent: bfloat16 [128, 256, 768], P(('wide', 'narrow')), may hold values from -6 to 6
- input_weight: bfloat16 [768, 2304], P(('wide', 'narrow')), may hold values from -0.21875 to 0.21875
- output_weight: bfloat16 [768, 768], P(('wide', 'narrow')), may hold values from -0.875 to 0.875
- expand_weight: bfloat16 [768, 3072], P(('wide', 'narrow')), may hold values from -0.21875 to 0.21875
- reduce_weight: bfloat16 [3072, 768], P(('wide', 'narrow')), may hold values from -0.15625 to 0.15625
- norm1_gain: bfloat16 [768], P(('wide', 'narrow')), may hold values from 0.5 to 1.5
- norm1_shift: bfloat16 [768], P(('wide', 'narrow')), may hold values from -1.75 to 1.75
- query_bias: bfloat16 [768], P(('wide', 'narrow')), may hold values from -3 to 3
- value_bias: bfloat16 [768], P(('wide', 'narrow')), may hold values from -1.75 to 1.75
- output_bias: bfloat16 [768], P(('wide', 'narrow')), may hold values from -1.75 to 1.75
- branch1_scale: bfloat16 [768], P(('wide', 'narrow')), may hold values from 0.29882812 to 1.5
- norm2_gain: bfloat16 [768], P(('wide', 'narrow')), may hold values from 0.5 to 1.5
- norm2_shift: bfloat16 [768], P(('wide', 'narrow')), may hold values from -1.75 to 1.75
- expand_bias: bfloat16 [3072], P(('wide', 'narrow')), may hold values from -3 to 3
- reduce_bias: bfloat16 [768], P(('wide', 'narrow')), may hold values from -1.75 to 1.75
- branch2_scale: bfloat16 [768], P(('wide', 'narrow')), may hold values from 0.29882812 to 1.5
Outputs:
- activations: bfloat16 [128, 256, 768], P(('wide', 'narrow'))
- input_grad: float32 [128, 256, 768], P(('wide', 'narrow'))
- input_weight_grad: float32 [768, 2304], P(('wide', 'narrow'))
- output_weight_grad: float32 [768, 768], P(('wide', 'narrow'))
- expand_weight_grad: float32 [768, 3072], P(('wide', 'narrow'))
- reduce_weight_grad: float32 [3072, 768], P(('wide', 'narrow'))
- norm1_gain_grad: float32 [768], P(('wide', 'narrow'))
- norm1_shift_grad: float32 [768], P(('wide', 'narrow'))
- query_bias_grad: float32 [768], P(('wide', 'narrow'))
- value_bias_grad: float32 [768], P(('wide', 'narrow'))
- output_bias_grad: float32 [768], P(('wide', 'narrow'))
- branch1_scale_grad: float32 [768], P(('wide', 'narrow'))
- norm2_gain_grad: float32 [768], P(('wide', 'narrow'))
- norm2_shift_grad: float32 [768], P(('wide', 'narrow'))
- expand_bias_grad: float32 [3072], P(('wide', 'narrow'))
- reduce_bias_grad: float32 [768], P(('wide', 'narrow'))
- branch2_scale_grad: float32 [768], P(('wide', 'narrow'))
Inputs may be any that keep to these rules, and one draw needn't show every extreme that they name: `counts`: valid patches of each image, heavy-tailed; every draw holds full images and images with only 16 valid patches.
All inputs are finite; a program needn't handle non-finite values.
Results may differ from a plain program's by a relative error of at most 0.015.
Values may be sent and summed in bfloat16 or wider, within the bound.
No kernel may reach another device: no remote copies, remote signals or barrier semaphores. Data moves between devices by JAX's collectives and lax.ppermute only.
A program may use at most 192 MiB of HBM per device.

v0:
```python
from functools import partial

import jax
import jax.numpy as jnp
from jax import lax
from jax.sharding import PartitionSpec as P

HEADS = 12
HEAD = 64


def layer_norm(inputs, norm_gain, norm_shift):
    average = jnp.mean(inputs, axis=-1, keepdims=True)
    centered = inputs - average
    spread = jnp.mean(centered * centered, axis=-1, keepdims=True)
    return centered * lax.rsqrt(spread + 1e-06) * norm_gain + norm_shift


def contract_rows(left, right):
    return lax.dot_general(
        left, right, (((0,), (0,)), ((), ())), preferred_element_type=jnp.float32
    )


def contract_cols(left, right):
    return lax.dot_general(
        left, right, (((1,), (1,)), ((), ())), preferred_element_type=jnp.float32
    )


def column_sum(values):
    return jnp.sum(values.astype(jnp.float32), axis=0)


def regroup(gradient, wide_count, narrow_count):
    total_rows = gradient.shape[0]
    piece_rows = total_rows // (wide_count * narrow_count)
    split = gradient.reshape((wide_count, narrow_count, piece_rows) + gradient.shape[1:])
    return jnp.swapaxes(split, 0, 1).reshape(gradient.shape)


def per_device(
    patches,
    counts,
    cotangent,
    input_weight,
    output_weight,
    expand_weight,
    reduce_weight,
    norm1_gain,
    norm1_shift,
    query_bias,
    value_bias,
    output_bias,
    branch1_scale,
    norm2_gain,
    norm2_shift,
    expand_bias,
    reduce_bias,
    branch2_scale,
):
    whole = (
        lax.all_gather(input_weight, ("wide", "narrow"), axis=0, tiled=True),
        lax.all_gather(output_weight, ("wide", "narrow"), axis=0, tiled=True),
        lax.all_gather(expand_weight, ("wide", "narrow"), axis=0, tiled=True),
        lax.all_gather(reduce_weight, ("wide", "narrow"), axis=0, tiled=True),
        lax.all_gather(norm1_gain, ("wide", "narrow"), axis=0, tiled=True),
        lax.all_gather(norm1_shift, ("wide", "narrow"), axis=0, tiled=True),
        lax.all_gather(query_bias, ("wide", "narrow"), axis=0, tiled=True),
        lax.all_gather(value_bias, ("wide", "narrow"), axis=0, tiled=True),
        lax.all_gather(output_bias, ("wide", "narrow"), axis=0, tiled=True),
        lax.all_gather(branch1_scale, ("wide", "narrow"), axis=0, tiled=True),
        lax.all_gather(norm2_gain, ("wide", "narrow"), axis=0, tiled=True),
        lax.all_gather(norm2_shift, ("wide", "narrow"), axis=0, tiled=True),
        lax.all_gather(expand_bias, ("wide", "narrow"), axis=0, tiled=True),
        lax.all_gather(reduce_bias, ("wide", "narrow"), axis=0, tiled=True),
        lax.all_gather(branch2_scale, ("wide", "narrow"), axis=0, tiled=True),
    )
    w_input, w_output, w_expand, w_reduce = (whole[0], whole[1], whole[2], whole[3])
    (
        gain_one,
        shift_one,
        bias_query,
        bias_value,
        bias_output,
        scale_one,
        gain_two,
        shift_two,
        bias_expand,
        bias_reduce,
        scale_two,
    ) = tuple((item.astype(jnp.float32) for item in whole[4:]))
    n_images, n_patch, width = patches.shape
    n_rows = n_images * n_patch
    head_shape = (n_images, n_patch, HEADS, HEAD)
    score_scale = HEAD ** (-0.5)
    position = jnp.arange(n_patch, dtype=jnp.int32)
    valid_keys = position[None, :] < counts[:, None]
    row_mask = jnp.where(valid_keys, 1.0, 0.0).astype(jnp.float32).reshape(n_rows, 1)
    rows_in = patches.astype(jnp.float32).reshape(n_rows, width)
    normed_low = layer_norm(rows_in, gain_one, shift_one).astype(jnp.bfloat16)
    projections = jnp.dot(normed_low, w_input, preferred_element_type=jnp.float32)
    queries = (projections[:, :width] + bias_query).astype(jnp.bfloat16).reshape(head_shape)
    key_rows = projections[:, width : 2 * width].astype(jnp.bfloat16).reshape(head_shape)
    values = (projections[:, 2 * width :] + bias_value).astype(jnp.bfloat16).reshape(head_shape)

    def attention_scores():
        raw_scores = jnp.einsum(
            "iphd,iqhd->ihpq", queries, key_rows, preferred_element_type=jnp.float32
        )
        return jnp.where(valid_keys[:, None, None, :], raw_scores * score_scale, -1e30)

    scores = attention_scores()
    log_total = jax.nn.logsumexp(scores, axis=-1, keepdims=True)
    soft_low = jnp.exp(scores - log_total).astype(jnp.bfloat16)
    attended = jnp.einsum("ihpq,iqhd->iphd", soft_low, values, preferred_element_type=jnp.float32)
    attended_low = attended.astype(jnp.bfloat16).reshape(n_rows, width)
    projected = jnp.dot(attended_low, w_output, preferred_element_type=jnp.float32) + bias_output
    middle = rows_in + scale_one * projected
    second_low = layer_norm(middle, gain_two, shift_two).astype(jnp.bfloat16)
    hidden = jnp.dot(second_low, w_expand, preferred_element_type=jnp.float32) + bias_expand
    activated_low = jax.nn.gelu(hidden, approximate=False).astype(jnp.bfloat16)
    branch = jnp.dot(activated_low, w_reduce, preferred_element_type=jnp.float32) + bias_reduce
    outputs = middle + scale_two * branch
    again = (
        lax.all_gather(input_weight, ("wide", "narrow"), axis=0, tiled=True),
        lax.all_gather(output_weight, ("wide", "narrow"), axis=0, tiled=True),
        lax.all_gather(expand_weight, ("wide", "narrow"), axis=0, tiled=True),
        lax.all_gather(reduce_weight, ("wide", "narrow"), axis=0, tiled=True),
    )
    back_input, back_output, back_expand, back_reduce = (again[0], again[1], again[2], again[3])
    grad_out = cotangent.astype(jnp.float32).reshape(n_rows, width) * row_mask
    grad_branch = (grad_out * scale_two).astype(jnp.bfloat16)
    grad_scale_two = jnp.sum(grad_out * branch, axis=0)
    grad_bias_reduce = column_sum(grad_branch)
    grad_w_reduce = contract_rows(activated_low, grad_branch)
    grad_activated = contract_cols(grad_branch, back_reduce)
    gelu_exact = partial(jax.nn.gelu, approximate=False)
    _, gelu_back = jax.vjp(gelu_exact, hidden)
    grad_hidden = gelu_back(grad_activated)[0].astype(jnp.bfloat16)
    grad_bias_expand = column_sum(grad_hidden)
    grad_w_expand = contract_rows(second_low, grad_hidden)
    grad_second = contract_cols(grad_hidden, back_expand)
    _, norm_back_two = jax.vjp(layer_norm, middle, gain_two, shift_two)
    grad_middle, grad_gain_two, grad_shift_two = norm_back_two(grad_second)
    grad_middle = grad_middle + grad_out
    grad_projected = (grad_middle * scale_one).astype(jnp.bfloat16)
    grad_scale_one = jnp.sum(grad_middle * projected, axis=0)
    grad_bias_output = column_sum(grad_projected)
    grad_w_output = contract_rows(attended_low, grad_projected)
    grad_attended = (
        contract_cols(grad_projected, back_output).astype(jnp.bfloat16).reshape(head_shape)
    )
    scores = attention_scores()
    soft_full = jnp.exp(scores - log_total)
    soft_again = soft_full.astype(jnp.bfloat16)
    grad_soft = jnp.einsum(
        "iphd,iqhd->ihpq", grad_attended, values, preferred_element_type=jnp.float32
    )
    grad_values = jnp.einsum(
        "ihpq,iphd->iqhd", soft_again, grad_attended, preferred_element_type=jnp.float32
    ).astype(jnp.bfloat16)
    grad_scores = (
        soft_full * (grad_soft - jnp.sum(soft_full * grad_soft, axis=-1, keepdims=True))
    ).astype(jnp.bfloat16)
    grad_queries = (
        (
            jnp.einsum("ihpq,iqhd->iphd", grad_scores, key_rows, preferred_element_type=jnp.float32)
            * score_scale
        )
        .astype(jnp.bfloat16)
        .reshape(n_rows, width)
    )
    grad_keys = (
        (
            jnp.einsum("ihpq,iphd->iqhd", grad_scores, queries, preferred_element_type=jnp.float32)
            * score_scale
        )
        .astype(jnp.bfloat16)
        .reshape(n_rows, width)
    )
    grad_values = grad_values.reshape(n_rows, width)
    grad_bias_query = column_sum(grad_queries)
    grad_bias_value = column_sum(grad_values)
    grad_projections = jnp.concatenate([grad_queries, grad_keys, grad_values], axis=1)
    grad_w_input = contract_rows(normed_low, grad_projections)
    grad_normed = contract_cols(grad_projections, back_input)
    _, norm_back_one = jax.vjp(layer_norm, rows_in, gain_one, shift_one)
    grad_rows, grad_gain_one, grad_shift_one = norm_back_one(grad_normed)
    input_grad = grad_rows + grad_middle
    wide_count = lax.axis_size("wide")
    narrow_count = lax.axis_size("narrow")
    (
        part_w_input,
        part_w_output,
        part_w_expand,
        part_w_reduce,
        part_gain_one,
        part_shift_one,
        part_bias_query,
        part_bias_value,
        part_bias_output,
        part_scale_one,
        part_gain_two,
        part_shift_two,
        part_bias_expand,
        part_bias_reduce,
        part_scale_two,
    ) = tuple(
        (
            regroup(item, wide_count, narrow_count)
            for item in (
                grad_w_input,
                grad_w_output,
                grad_w_expand,
                grad_w_reduce,
                grad_gain_one,
                grad_shift_one,
                grad_bias_query,
                grad_bias_value,
                grad_bias_output,
                grad_scale_one,
                grad_gain_two,
                grad_shift_two,
                grad_bias_expand,
                grad_bias_reduce,
                grad_scale_two,
            )
        )
    )
    inner = (
        lax.psum_scatter(
            part_w_input.astype(jnp.bfloat16), "narrow", scatter_dimension=0, tiled=True
        ).astype(jnp.float32),
        lax.psum_scatter(
            part_w_output.astype(jnp.bfloat16), "narrow", scatter_dimension=0, tiled=True
        ).astype(jnp.float32),
        lax.psum_scatter(
            part_w_expand.astype(jnp.bfloat16), "narrow", scatter_dimension=0, tiled=True
        ).astype(jnp.float32),
        lax.psum_scatter(
            part_w_reduce.astype(jnp.bfloat16), "narrow", scatter_dimension=0, tiled=True
        ).astype(jnp.float32),
        lax.psum_scatter(
            part_gain_one.astype(jnp.bfloat16), "narrow", scatter_dimension=0, tiled=True
        ).astype(jnp.float32),
        lax.psum_scatter(
            part_shift_one.astype(jnp.bfloat16), "narrow", scatter_dimension=0, tiled=True
        ).astype(jnp.float32),
        lax.psum_scatter(
            part_bias_query.astype(jnp.bfloat16), "narrow", scatter_dimension=0, tiled=True
        ).astype(jnp.float32),
        lax.psum_scatter(
            part_bias_value.astype(jnp.bfloat16), "narrow", scatter_dimension=0, tiled=True
        ).astype(jnp.float32),
        lax.psum_scatter(
            part_bias_output.astype(jnp.bfloat16), "narrow", scatter_dimension=0, tiled=True
        ).astype(jnp.float32),
        lax.psum_scatter(
            part_scale_one.astype(jnp.bfloat16), "narrow", scatter_dimension=0, tiled=True
        ).astype(jnp.float32),
        lax.psum_scatter(
            part_gain_two.astype(jnp.bfloat16), "narrow", scatter_dimension=0, tiled=True
        ).astype(jnp.float32),
        lax.psum_scatter(
            part_shift_two.astype(jnp.bfloat16), "narrow", scatter_dimension=0, tiled=True
        ).astype(jnp.float32),
        lax.psum_scatter(
            part_bias_expand.astype(jnp.bfloat16), "narrow", scatter_dimension=0, tiled=True
        ).astype(jnp.float32),
        lax.psum_scatter(
            part_bias_reduce.astype(jnp.bfloat16), "narrow", scatter_dimension=0, tiled=True
        ).astype(jnp.float32),
        lax.psum_scatter(
            part_scale_two.astype(jnp.bfloat16), "narrow", scatter_dimension=0, tiled=True
        ).astype(jnp.float32),
    )
    summed = (
        lax.psum_scatter(inner[0], "wide", scatter_dimension=0, tiled=True),
        lax.psum_scatter(inner[1], "wide", scatter_dimension=0, tiled=True),
        lax.psum_scatter(inner[2], "wide", scatter_dimension=0, tiled=True),
        lax.psum_scatter(inner[3], "wide", scatter_dimension=0, tiled=True),
        lax.psum_scatter(inner[4], "wide", scatter_dimension=0, tiled=True),
        lax.psum_scatter(inner[5], "wide", scatter_dimension=0, tiled=True),
        lax.psum_scatter(inner[6], "wide", scatter_dimension=0, tiled=True),
        lax.psum_scatter(inner[7], "wide", scatter_dimension=0, tiled=True),
        lax.psum_scatter(inner[8], "wide", scatter_dimension=0, tiled=True),
        lax.psum_scatter(inner[9], "wide", scatter_dimension=0, tiled=True),
        lax.psum_scatter(inner[10], "wide", scatter_dimension=0, tiled=True),
        lax.psum_scatter(inner[11], "wide", scatter_dimension=0, tiled=True),
        lax.psum_scatter(inner[12], "wide", scatter_dimension=0, tiled=True),
        lax.psum_scatter(inner[13], "wide", scatter_dimension=0, tiled=True),
        lax.psum_scatter(inner[14], "wide", scatter_dimension=0, tiled=True),
    )
    return (
        outputs.reshape(n_images, n_patch, width).astype(jnp.bfloat16),
        input_grad.reshape(n_images, n_patch, width),
        summed[0],
        summed[1],
        summed[2],
        summed[3],
        summed[4],
        summed[5],
        summed[6],
        summed[7],
        summed[8],
        summed[9],
        summed[10],
        summed[11],
        summed[12],
        summed[13],
        summed[14],
    )


def solution(mesh):
    placed = (
        P(("wide", "narrow"), None, None),
        P(("wide", "narrow")),
        P(("wide", "narrow"), None, None),
        P(("wide", "narrow"), None),
        P(("wide", "narrow"), None),
        P(("wide", "narrow"), None),
        P(("wide", "narrow"), None),
        P(("wide", "narrow")),
        P(("wide", "narrow")),
        P(("wide", "narrow")),
        P(("wide", "narrow")),
        P(("wide", "narrow")),
        P(("wide", "narrow")),
        P(("wide", "narrow")),
        P(("wide", "narrow")),
        P(("wide", "narrow")),
        P(("wide", "narrow")),
        P(("wide", "narrow")),
    )
    return jax.shard_map(
        per_device,
        mesh=mesh,
        in_specs=placed,
        out_specs=(
            P(("wide", "narrow"), None, None),
            P(("wide", "narrow"), None, None),
            P(("wide", "narrow"), None),
            P(("wide", "narrow"), None),
            P(("wide", "narrow"), None),
            P(("wide", "narrow"), None),
            P(("wide", "narrow")),
            P(("wide", "narrow")),
            P(("wide", "narrow")),
            P(("wide", "narrow")),
            P(("wide", "narrow")),
            P(("wide", "narrow")),
            P(("wide", "narrow")),
            P(("wide", "narrow")),
            P(("wide", "narrow")),
            P(("wide", "narrow")),
            P(("wide", "narrow")),
        ),
        check_vma=False,
    )
```

profile of v0, /device:TPU:0, one launch (start us, length us, event | category | flops | bytes accessed | tf_op | source)
XLA Modules:
  0.0 793.1 jit_solution(13559499145613062602)
XLA Ops:
  25.2 43.4 %all-reduce.34 = (bf16[768]{0:T(1024)(128)(2,1)S(1)}, bf16[768]{0:T(1024)(128)(2,1)S(1)}, bf16[768]{0:T(1024)(128)(2,1)S(1)}, bf16[768]{0:T(1024)(128)(2,1)S(1)}...) all-reduce(bf16[768]{0:T(1024)(128)(2,1)S(1)} %dynamic-update-slice, ...), channel_id=1, replica_groups=mesh['wide'=8,'narrow'=4] {'wide','narrow'}, use_global_device_ids=true, to_apply=%add.2 | all-reduce | flops 10752 | bytes 43008
  70.6 2.6 copy.142
  74.8 6.3 fusion.90
  85.8 2.9 reshape.301
  88.7 3.2 copy.121
  91.9 3.9 reshape.302
  95.8 2.6 copy.119
  98.4 3.9 reshape.300
  102.2 4.5 fusion.23
  106.8 3.9 exponential_reduce_fusion
  111.5 3.5 fusion.51
  116.7 12.8 %all-gather.7.cloned.1.call-done = bf16[768,768]{1,0:T(8,128)(2,1)} async-done(((bf16[24,768]{1,0:T(8,128)(2,1)}), bf16[768,768]{1,0:T(8,128)(2,1)}) %all-gather.7.cloned.1.call-update) | async-done | bytes 1179664 | tf_op jit(solution)/shard_map/all_gather | solution.py:64
  129.5 4.6 fusion.86
  136.4 58.6 %all-gather.9.cloned.1.call-done = bf16[768,3072]{1,0:T(8,128)(2,1)} async-done(((bf16[24,3072]{1,0:T(8,128)(2,1)}), bf16[768,3072]{1,0:T(8,128)(2,1)}) %all-gather.9.cloned.1.call-update) | async-done | bytes 4718608 | tf_op jit(solution)/shard_map/all_gather | solution.py:65
  194.9 36.6 %fusion = (f32[1024,3072]{1,0:T(8,128)}, f32[1024,3072]{1,0:T(8,128)}) fusion(f32[3072]{0:T(1024)S(1)} %convert_element_type.344, bf16[768,3072]{1,0:T(8,128)(2,1)} %all-gather.9.cloned.1.call-done, f32[1024,768]{1,0:T(8,128)} %copy-done.8, f32[768]{0:T(1024)S(1)} %convert_element_type.342, f32[768]{0:T(1024)S(1)} %convert_element_type.341, ...), kind=kOutput, calls=%fused_computation.2 | convolution fusion | flops 5033951232 | bytes 33056768 | tf_op jit(solution)/shard_map/dot_general | solution.py:121
  231.5 28.1 %all-gather.11.cloned.1.call-done = bf16[3072,768]{1,0:T(8,128)(2,1)} async-done(((bf16[96,768]{1,0:T(8,128)(2,1)}), bf16[3072,768]{1,0:T(8,128)(2,1)}) %all-gather.11.cloned.1.call-update) | async-done | bytes 4718608 | tf_op jit(solution)/shard_map/all_gather | solution.py:66
  259.7 16.9 %fusion.89 = (bf16[3072]{0:T(1024)(128)(2,1)S(1)}, bf16[1024,3072]{1,0:T(8,128)(2,1)}) fusion(f32[1024,3072]{1,0:T(8,128)} %get-tuple-element.78, bf16[1024,768]{1,0:T(8,128)(2,1)S(1)} %copy-done.15, bf16[3072,768]{1,0:T(8,128)(2,1)} %all-gather.11.cloned.1.call-done, f32[1024,3072]{1,0:T(8,128)} %get-tuple-element.79, f32[3072]{0:T(1024)S(1)} %convert_element_type.344), kind=kOutput, calls=%fused_computation.157 | convolution fusion | flops 4882166784 | bytes 37767168 | tf_op jit(solution)/shard_map/dot_general | solution.py:26
  276.5 9.4 %multiply_reduce_fusion.2 = (bf16[768]{0:T(1024)(128)(2,1)S(1)}, f32[1024]{0:T(1024)S(1)}, bf16[768]{0:T(1024)(128)(2,1)S(1)}, f32[1024,768]{1,0:T(8,128)S(1)}) fusion(f32[1024,768]{1,0:T(8,128)S(1)} %copy-done.9, f32[1024]{0:T(1024)S(1)} %fusion.70, f32[1024]{0:T(1024)S(1)} %broadcast_multiply_fusion, f32[768]{0:T(1024)S(1)} %convert_element_type.341, ...), kind=kOutput, calls=%fused_computation.80 | convolution fusion | flops 4838126592 | bytes 17319936 | tf_op jit(solution)/shard_map/dot_general | solution.py:26
  292.6 4.3 convolution_convert_fusion.4
  296.9 3.0 copy.127
  300.0 3.9 reshape.305
  303.8 11.0 %multiply_reduce_fusion = (f32[4,12,256]{2,1,0:T(8,128)S(1)}, f32[4,12,256,256]{2,3,1,0:T(8,128)}) fusion(f32[4,12,256,256]{2,3,1,0:T(8,128)} %copy-done, f32[4,12,256]{2,1,0:T(8,128)S(1)} %log_add_fusion, pred[4,256]{1,0:T(4,128)(4,1)S(1)} %iota_compare_fusion, bf16[4,256,12,64]{1,0,3,2:T(4,128)(2,1)S(1)} %copy-done.12, bf16[4,256,12,64]{1,0,3,2:T(4,128)(2,1)} %reshape.305), kind=kOutput, calls=%fused_computation.24 | convolution fusion | flops 418369536 | bytes 28410880 | tf_op jit(solution)/shard_map/iphd,iqhd->ihpq/dot_general | solution.py:157
  314.8 13.4 %multiply_convert_fusion = bf16[4,12,256,256]{2,3,1,0:T(8,128)(2,1)} fusion(f32[4,12,256,256]{2,3,1,0:T(8,128)} %get-tuple-element.82, f32[4,12,256,256]{2,3,1,0:T(8,128)} %copy-done, f32[4,12,256]{2,1,0:T(8,128)S(1)} %get-tuple-element.81, f32[4,12,256]{2,1,0:T(8,128)S(1)} %log_add_fusion, pred[4,256]{1,0:T(4,128)(4,1)S(1)} %iota_compare_fusion), kind=kLoop, calls=%fused_computation.23 | loop fusion | flops 18874368 | bytes 31556608 | tf_op jit(solution)/shard_map/convert_element_type | solution.py:165
  328.3 3.4 fusion.88
  334.4 2.6 copy.141
  337.0 4.8 fusion.54
  344.6 2.8 copy.140
  347.4 4.1 fusion.87
  355.9 6.7 fusion.29
  364.8 9.0 %convolution_convert_fusion = bf16[768,3072]{1,0:T(8,128)(2,1)S(1)} fusion(bf16[1024,3072]{1,0:T(8,128)(2,1)} %get-tuple-element.89, f32[1024,768]{1,0:T(8,128)} %copy-done.8, f32[768]{0:T(1024)S(1)} %convert_element_type.342, f32[768]{0:T(1024)S(1)} %convert_element_type.341, f32[1024]{0:T(1024)S(1)} %fusion.70, f32[1024]{0:T(1024)S(1)} %broadcast_multiply_fusion), kind=kOutput, calls=%fused_computation.50 | convolution fusion | flops 4838129664 | bytes 14170112 | tf_op jit(solution)/shard_map/dot_general | solution.py:20
  373.7 2.5 copy.145
  377.5 30.5 %fusion.3 = bf16[3072,1024]{0,1:T(8,128)(2,1)} fusion(f32[1024,3072]{1,0:T(8,128)} %get-tuple-element.79, f32[3072]{0:T(1024)S(1)} %convert_element_type.344), kind=kLoop, calls=%fused_computation.5 | loop fusion | flops 207618048 | bytes 18886656 | tf_op jit(solution)/shard_map/convert_element_type | solution.py:122
  408.0 8.9 %copy.146 = bf16[3072,1024]{1,0:T(8,128)(2,1)} copy(bf16[3072,1024]{0,1:T(8,128)(2,1)} %fusion.3) | data formatting | bytes 12582912 | tf_op jit(solution)/shard_map/convert_element_type | solution.py:122
  417.0 8.4 %convert_bitcast_fusion = bf16[4,8,96,768]{3,2,0,1:T(8,128)(2,1)S(1)} fusion(bf16[8,4,96,1024]{3,2,1,0:T(8,128)(2,1)} %bitcast.228, bf16[1024,768,1,1]{1,0,3,2:T(8,128)(2,1)S(1)} %bitcast.242), kind=kOutput, calls=%fused_computation.56 | convolution fusion | flops 4834197504 | bytes 12582912 | tf_op jit(solution)/shard_map/dot_general | solution.py:20
  425.4 2.5 copy.147
  430.0 2.6 convert_element_type.364
  432.6 21.4 %reduce-scatter.17.cloned.1.call-done = bf16[192,3072]{1,0:T(8,128)(2,1)} async-done(((bf16[768,3072]{1,0:T(8,128)(2,1)}), bf16[192,3072]{1,0:T(8,128)(2,1)}) %reduce-scatter.17.cloned.1.call-update) | async-done | bytes 1179664 | tf_op jit(solution)/shard_map/reduce_scatter | solution.py:238
  454.1 2.9 convert_element_type.373
  461.1 10.3 %fusion.82 = (bf16[768]{0:T(1024)(128)(2,1)S(1)}, f32[1024]{0:T(1024)S(1)}, f32[1024,768]{1,0:T(8,128)}) fusion(f32[768]{0:T(1024)S(1)} %copy-done.24, f32[1024]{0:T(1024)S(1)} %bitcast.244, bf16[4,256,768]{2,1,0:T(8,128)(2,1)S(1)} %copy-done.2, bf16[768,2304]{1,0:T(8,128)(2,1)} %all-gather.5.cloned.1.call-done, bf16[1024,768]{1,0:T(8,128)(2,1)} %copy.141, ...), kind=kOutput, calls=%fused_computation.150 | convolution fusion | flops 3642751232 | bytes 12988928 | tf_op jit(solution)/shard_map/dot_general | solution.py:26
  471.5 33.1 %reduce-scatter.21.cloned.1.call-done = bf16[768,768]{1,0:T(8,128)(2,1)} async-done(((bf16[3072,768]{1,0:T(8,128)(2,1)}), bf16[768,768]{1,0:T(8,128)(2,1)}) %reduce-scatter.21.cloned.1.call-update) | async-done | bytes 1179664 | tf_op jit(solution)/shard_map/reduce_scatter | solution.py:241
  504.6 2.9 convert_element_type.380
  507.5 3.2 fusion.41
  512.1 20.1 %multiply_reduce_fusion.1 = (bf16[768]{0:T(1024)(128)(2,1)S(1)}, bf16[768]{0:T(1024)(128)(2,1)S(1)}, f32[1024,768]{1,0:T(8,128)}, bf16[1024,768]{1,0:T(8,128)(2,1)}) fusion(bf16[4,256,768]{2,1,0:T(8,128)(2,1)S(1)} %copy-done.6, f32[1024]{0:T(1024)S(1)} %bitcast.249, f32[768]{0:T(1024)S(1)} %convert_element_type.346, f32[1024,768]{1,0:T(8,128)} %get-tuple-element.77, ...), kind=kOutput, calls=%fused_computation.79 | convolution fusion | flops 4861720576 | bytes 50383872 | tf_op jit(solution)/shard_map/dot_general | solution.py:123
  532.9 10.9 %all-reduce.35 = (bf16[768]{0:T(1024)(128)(2,1)S(1)}, bf16[768]{0:T(1024)(128)(2,1)S(1)}, bf16[768]{0:T(1024)(128)(2,1)S(1)}, bf16[768]{0:T(1024)(128)(2,1)S(1)}...) all-reduce(bf16[768]{0:T(1024)(128)(2,1)S(1)} %convert_element_type, ...), channel_id=10, replica_groups=mesh['wide'=8,'narrow'=4] {'narrow'}, use_global_device_ids=true, to_apply=%region_20.21.clone | all-reduce | flops 10752 | bytes 43008
  544.2 36.8 %all-reduce.33 = (f32[192]{0:T(256)S(1)}, f32[192]{0:T(256)S(1)}, f32[192]{0:T(256)S(1)}, f32[192]{0:T(256)S(1)}, f32[192]{0:T(256)S(1)}, /*index=5*/f32[192]{0:...) all-reduce(f32[192]{0:T(256)S(1)} %get-tuple-element.99, ...), channel_id=11, replica_groups=mesh['wide'=8,'narrow'=4] {'wide'}, use_global_device_ids=true, to_apply=%region_21.22.clone | all-reduce | flops 2688 | bytes 21504
  587.4 53.4 %reduce-scatter.11.cloned.1.call-done = f32[24,2304]{1,0:T(8,128)} async-done(((f32[192,2304]{1,0:T(8,128)}), f32[24,2304]{1,0:T(8,128)}) %reduce-scatter.11.cloned.1.call-update) | async-done | bytes 221200 | tf_op jit(solution)/shard_map/reduce_scatter | solution.py:279
  640.7 72.5 %reduce-scatter.19.cloned.1.call-done = f32[24,3072]{1,0:T(8,128)} async-done(((f32[192,3072]{1,0:T(8,128)}), f32[24,3072]{1,0:T(8,128)}) %reduce-scatter.19.cloned.1.call-update) | async-done | bytes 294928 | tf_op jit(solution)/shard_map/reduce_scatter | solution.py:281
  713.3 72.8 %reduce-scatter.23.cloned.1.call-done = f32[96,768]{1,0:T(8,128)} async-done(((f32[768,768]{1,0:T(8,128)}), f32[96,768]{1,0:T(8,128)}) %reduce-scatter.23.cloned.1.call-update) | async-done | bytes 294928 | tf_op jit(solution)/shard_map/reduce_scatter | solution.py:282
  (234 shorter events, 62.8 us)
Async XLA Ops:
  7.2 61.6 %copy-start.1 = (bf16[4,256,768]{2,1,0:T(8,128)(2,1)S(1)}, bf16[4,256,768]{2,1,0:T(8,128)(2,1)}, u32[]{:S(2)}) copy-start(bf16[4,256,768]{2,1,0:T(8,128)(2,1)} %param.18) | copy-start | bytes 4718596
  7.2 67.6 %all-gather.5.cloned.1.call-start = ((), (), s32[]{:S(2)}) async-start(), calls=%async_computation.8 | async-start | bytes 3649536 | tf_op jit(solution)/shard_map/all_gather | solution.py:63
  7.9 121.6 %all-gather.7.cloned.1.call-start = ((), (), s32[]{:S(2)}) async-start(), calls=%async_computation.9 | async-start | bytes 1216512 | tf_op jit(solution)/shard_map/all_gather | solution.py:64
  8.7 186.3 %all-gather.9.cloned.1.call-start = ((), (), s32[]{:S(2)}) async-start(), calls=%async_computation.10 | async-start | bytes 4866048 | tf_op jit(solution)/shard_map/all_gather | solution.py:65
  9.4 250.2 %all-gather.11.cloned.1.call-start = ((), (), s32[]{:S(2)}) async-start(), calls=%async_computation.11 | async-start | bytes 4866048 | tf_op jit(solution)/shard_map/all_gather | solution.py:66
  10.0 418.0 %reduce-scatter.13.cloned.1.call-start = ((), (), s32[]{:S(2)}) async-start(), calls=%async_computation.14 | async-start | bytes 1474560 | tf_op jit(solution)/shard_map/reduce_scatter | solution.py:235
  12.1 61.1 %copy-start.5 = (bf16[4,256,768]{2,1,0:T(8,128)(2,1)S(1)}, bf16[4,256,768]{2,1,0:T(8,128)(2,1)}, u32[]{:S(2)}) copy-start(bf16[4,256,768]{2,1,0:T(8,128)(2,1)} %param.20) | copy-start | bytes 4718596
  13.9 60.8 %copy-start.19 = (f32[1,2,4,128]{3,1,2,0:T(2,128)}, f32[1,2,4,128]{3,1,2,0:T(2,128)S(1)}, u32[]{:S(2)}) copy-start(f32[1,2,4,128]{3,1,2,0:T(2,128)S(1)} %copy.166) | copy-start | bytes 12292
  15.9 52.7 %copy-start.29 = (f32[1,2,4,128]{3,1,2,0:T(2,128)}, f32[1,2,4,128]{3,1,2,0:T(2,128)S(1)}, u32[]{:S(2)}) copy-start(f32[1,2,4,128]{3,1,2,0:T(2,128)S(1)} %copy.167) | copy-start | bytes 12292
  16.0 58.8 %copy-start.21 = (f32[1024]{0:T(1024)}, f32[1024]{0:T(1024)S(1)}, u32[]{:S(2)}) copy-start(f32[1024]{0:T(1024)S(1)} %rsqrt.22) | copy-start | bytes 12292
  68.6 6.1 copy-start.23
  68.7 6.1 copy-start.25
  68.7 60.8 %copy-start.32 = (f32[768]{0:T(1024)}, f32[768]{0:T(1024)S(1)}, u32[]{:S(2)}) copy-start(f32[768]{0:T(1024)S(1)} %convert_element_type.339) | copy-start | bytes 9220
  68.7 6.0 copy-start.27
  88.7 13.5 %copy-start.3 = (bf16[4,256,12,64]{1,0,3,2:T(4,128)(2,1)}, bf16[4,256,12,64]{1,0,3,2:T(4,128)(2,1)S(1)}, u32[]{:S(2)}) copy-start(bf16[4,256,12,64]{1,0,3,2:T(4,128)(2,1)S(1)} %reshape.301) | copy-start | bytes 4718596
  106.8 4.7 copy-start
  106.8 4.7 copy-start.11
  116.7 17.5 %copy-start.16 = (bf16[96,8,4,256]{3,1,2,0:T(8,128)(2,1)}, bf16[96,8,4,256]{3,1,2,0:T(8,128)(2,1)S(1)}, u32[]{:S(2)}) copy-start(bf16[96,8,4,256]{3,1,2,0:T(8,128)(2,1)S(1)} %copy.168) | copy-start | bytes 4718596
  134.1 1.7 copy-start.8
  136.4 123.3 %copy-start.15 = (bf16[1024,768]{1,0:T(8,128)(2,1)S(1)}, bf16[1024,768]{1,0:T(8,128)(2,1)}, u32[]{:S(2)}) copy-start(bf16[1024,768]{1,0:T(8,128)(2,1)} %multiply_convert_fusion.7) | copy-start | bytes 4718596
  259.7 16.9 %copy-start.9 = (f32[1024,768]{1,0:T(8,128)S(1)}, f32[1024,768]{1,0:T(8,128)}, u32[]{:S(2)}) copy-start(f32[1024,768]{1,0:T(8,128)} %copy-done.8) | copy-start | bytes 9437188
  287.4 4.0 copy-start.10
  287.4 2.6 copy-start.17
  288.2 4.3 copy-start.18
  292.6 137.4 %reduce-scatter.9.cloned.1.call-start = ((), (), s32[]{:S(2)}) async-start(), calls=%async_computation.12 | async-start | bytes 4423680 | tf_op jit(solution)/shard_map/reduce_scatter | solution.py:232
  296.9 6.9 copy-start.12
  303.8 24.4 %slice-start = ((s8[12582912]{0:T(1024)(128)(4,1)}), s8[4194304]{0:T(1024)(128)(4,1)S(1)}, s32[]{:S(2)}) async-start(s8[12582912]{0:T(1024)(128)(4,1)} %bitcast.223), calls=%async_computation.20 | async-start | bytes 8388608
  303.8 24.4 %slice-start.1 = ((s8[12582912]{0:T(1024)(128)(4,1)}), s8[4194304]{0:T(1024)(128)(4,1)S(1)}, s32[]{:S(2)}) async-start(s8[12582912]{0:T(1024)(128)(4,1)} %bitcast.223), calls=%async_computation.21 | async-start | bytes 8388608
  314.8 13.4 %slice-start.2 = ((s8[12582912]{0:T(1024)(128)(4,1)}), s8[4194304]{0:T(1024)(128)(4,1)S(1)}, s32[]{:S(2)}) async-start(s8[12582912]{0:T(1024)(128)(4,1)} %bitcast.223), calls=%async_computation.22 | async-start | bytes 8388608
  314.8 13.4 %copy-start.13 = (bf16[4,256,12,64]{1,0,3,2:T(4,128)(2,1)S(1)}, bf16[4,256,12,64]{1,0,3,2:T(4,128)(2,1)}, u32[]{:S(2)}) copy-start(bf16[4,256,12,64]{1,0,3,2:T(4,128)(2,1)} %reshape.305) | copy-start | bytes 4718596
  331.7 5.3 copy-start.4
  341.8 5.5 copy-start.7
  355.9 6.8 copy-start.14
  364.7 89.4 %reduce-scatter.17.cloned.1.call-start = ((), (), s32[]{:S(2)}) async-start(), calls=%async_computation.16 | async-start | bytes 5898240 | tf_op jit(solution)/shard_map/reduce_scatter | solution.py:238
  376.3 128.3 %reduce-scatter.21.cloned.1.call-start = ((), (), s32[]{:S(2)}) async-start(), calls=%async_computation.18 | async-start | bytes 5898240 | tf_op jit(solution)/shard_map/reduce_scatter | solution.py:241
  427.9 159.5 %reduce-scatter.15.cloned.1.call-start = ((), (), s32[]{:S(2)}) async-start(), calls=%async_computation.15 | async-start | bytes 663552 | tf_op jit(solution)/shard_map/reduce_scatter | solution.py:280
  429.8 27.2 %copy-start.36 = (u32[32]{0:T(128)S(1)}, u32[32]{0:T(128)}, u32[]{:S(2)}) copy-start(u32[32]{0:T(128)} %constant.159) | copy-start | bytes 388
  429.8 29.1 %copy-start.35 = (u32[32]{0:T(128)S(1)}, u32[32]{0:T(128)}, u32[]{:S(2)}) copy-start(u32[32]{0:T(128)} %constant.155) | copy-start | bytes 388
  429.9 31.0 %copy-start.34 = (bf16[768]{0:T(1024)(128)(2,1)S(1)}, bf16[768]{0:T(1024)(128)(2,1)}, u32[]{:S(2)}) copy-start(bf16[768]{0:T(1024)(128)(2,1)} %get-tuple-element.46) | copy-start | bytes 4612
  429.9 31.2 %copy-start.2 = (bf16[4,256,768]{2,1,0:T(8,128)(2,1)S(1)}, bf16[4,256,768]{2,1,0:T(8,128)(2,1)}, u32[]{:S(2)}) copy-start(bf16[4,256,768]{2,1,0:T(8,128)(2,1)} %param.18) | copy-start | bytes 4718596
  429.9 31.2 %copy-start.20 = (f32[1,2,4,128]{3,1,2,0:T(2,128)S(1)}, f32[1,2,4,128]{3,1,2,0:T(2,128)}, u32[]{:S(2)}) copy-start(f32[1,2,4,128]{3,1,2,0:T(2,128)} %copy-done.19) | copy-start | bytes 12292
  429.9 31.2 %copy-start.24 = (f32[768]{0:T(1024)S(1)}, f32[768]{0:T(1024)}, u32[]{:S(2)}) copy-start(f32[768]{0:T(1024)} %copy-done.23) | copy-start | bytes 9220
  429.9 210.8 %reduce-scatter.11.cloned.1.call-start = ((), (), s32[]{:S(2)}) async-start(), calls=%async_computation.13 | async-start | bytes 1990656 | tf_op jit(solution)/shard_map/reduce_scatter | solution.py:279
  432.6 280.7 %reduce-scatter.19.cloned.1.call-start = ((), (), s32[]{:S(2)}) async-start(), calls=%async_computation.17 | async-start | bytes 2654208 | tf_op jit(solution)/shard_map/reduce_scatter | solution.py:281
  457.0 329.1 %reduce-scatter.23.cloned.1.call-start = ((), (), s32[]{:S(2)}) async-start(), calls=%async_computation.19 | async-start | bytes 2654208 | tf_op jit(solution)/shard_map/reduce_scatter | solution.py:282
  461.1 10.3 %copy-start.30 = (f32[1,2,4,128]{3,1,2,0:T(2,128)S(1)}, f32[1,2,4,128]{3,1,2,0:T(2,128)}, u32[]{:S(2)}) copy-start(f32[1,2,4,128]{3,1,2,0:T(2,128)} %copy-done.29) | copy-start | bytes 12292
  471.4 36.0 %copy-start.22 = (f32[1024]{0:T(1024)S(1)}, f32[1024]{0:T(1024)}, u32[]{:S(2)}) copy-start(f32[1024]{0:T(1024)} %copy-done.21) | copy-start | bytes 12292
  471.4 40.6 %copy-start.33 = (f32[768]{0:T(1024)S(1)}, f32[768]{0:T(1024)}, u32[]{:S(2)}) copy-start(f32[768]{0:T(1024)} %copy-done.32) | copy-start | bytes 9220
  (4 other events, 4.5 us)
Sparse Core Ops, SparseCore 0:
  10.9 62.9 all-gather.4
  76.8 52.6 all-gather.6
  132.4 62.4 all-gather.8
  197.7 61.9 all-gather.10
  292.7 23.8 reduce-scatter.12
  364.8 38.6 reduce-scatter.8
  406.1 47.9 reduce-scatter.16
  456.6 47.9 reduce-scatter.20
  508.4 62.6 reduce-scatter.14
  575.1 65.6 reduce-scatter.10
  644.8 68.4 reduce-scatter.18
  717.2 68.8 reduce-scatter.22
where the time goes:
time: 798 us; the launch traced here: 793 us
  waiting for transfers between devices  356 us (45%)
  matrix products  165 us (21%)
  blocking collectives  91.1 us (11%)
  local copies, waits for them, and re-layouts  86.7 us (11%)
  other arithmetic  76 us (10%)
  between operations  17.9 us (2%)
    unnamed x3, blocking collectives  91.1 us
    reduce_scatter x1, waiting for transfers between devices, per_device(): lax.psum_scatter(inner[3], 'wide', scatter_dimension=0, tiled=True)  72.8 us
    reduce_scatter x1, waiting for transfers between devices, per_device(): lax.psum_scatter(inner[2], 'wide', scatter_dimension=0, tiled=True)  72.5 us
    all_gather x1, waiting for transfers between devices, per_device(): lax.all_gather(expand_weight, ('wide', 'narrow'), axis=0, tiled=True)  58.6 us
    reduce_scatter x1, waiting for transfers between devices, per_device(): lax.psum_scatter(inner[0], 'wide', scatter_dimension=0, tiled=True)  53.4 us
    dot_general x4, matrix products, contract_cols(): lax.dot_general(left, right, (((1,), (1,)), ((), ())), preferred_element_...  40.9 us
    dot_general x1, matrix products, per_device(): jnp.dot(second_low, w_expand, preferred_element_type=jnp.float32)  36.6 us
    reduce_scatter x1, waiting for transfers between devices, per_device(): lax.psum_scatter(part_w_reduce.astype(jnp.bfloat16), 'narrow', scatter_di...  33.1 us
  transfers between devices with their start and end apart: 12, of which 8 were waited for; matrix products, arithmetic and copies ran while one was open for 37% of the time, Pallas kernels for 0%

commit v1 on v0

v1 whole, which is shorter than its diff:
```python
from functools import partial

import jax
import jax.numpy as jnp
from jax import lax
from jax.sharding import PartitionSpec as P

HEADS = 12
HEAD = 64
AXES = ("wide", "narrow")
LANES = 128


def shuffle(value, count, target):
    return lax.ppermute(value, AXES, [(d, target(d)) for d in range(count)])

def digits(planes):
    radices = []
    while planes > 1:
        radix = 4 if planes % 4 == 0 else 2 if planes % 2 == 0 else planes
        radices.append(radix)
        planes //= radix
    return radices


def shifted(device, stride, radix, step):
    digit = (device // stride) % radix
    return device + (((digit + step) % radix) - digit) * stride


def gather_z(shard, count):
    me = lax.axis_index(AXES)
    held = shard[None]
    stride = 8
    for radix in digits(count // 8):
        mine = (me // stride) % radix
        out = jnp.zeros((radix,) + held.shape, held.dtype)
        pieces = [held] + [
            shuffle(held, count, lambda d, s=s: shifted(d, stride, radix, s))
            for s in range(1, radix)
        ]
        for s, piece in enumerate(pieces):
            out = lax.dynamic_update_index_in_dim(out, piece, (mine - s) % radix, 0)
        held = out.reshape((-1,) + shard.shape)
        stride *= radix
    return held


def gather_xy(plane, count):
    planes = plane.shape[0]
    half = planes // 2
    across_x = shuffle(plane, count, lambda d: d ^ 2)
    across_y = shuffle(plane, count, lambda d: d ^ 4)
    far_a = shuffle(across_y[:half], count, lambda d: d ^ 2)
    far_b = shuffle(across_x[half:], count, lambda d: d ^ 4)
    return plane, across_x, across_y, far_a, far_b

def assemble(pieces, count):
    plane, across_x, across_y, far_a, far_b = pieces
    planes, rows, cols = plane.shape
    half = planes // 2
    me = lax.axis_index(AXES)
    core = me % 2
    spot = (me // 2) % 4
    held = jnp.zeros((planes, 4, rows, cols), plane.dtype)
    def put(buf, item, z, yx):
        return lax.dynamic_update_slice(buf, item[:, None], (z, yx, 0, 0))
    held = put(held, plane, 0, spot)
    held = put(held, across_x, 0, spot ^ 1)
    held = put(held, across_y, 0, spot ^ 2)
    held = put(held, far_a, 0, spot ^ 3)
    held = put(held, far_b, half, spot ^ 3)
    other = shuffle(held, count, lambda d: d ^ 1)
    full = jnp.zeros((planes, 4, 2, rows, cols), plane.dtype)
    full = lax.dynamic_update_slice(full, held[:, :, None], (0, 0, core, 0, 0))
    full = lax.dynamic_update_slice(full, other[:, :, None], (0, 0, 1 - core, 0, 0))
    return full.reshape(count * rows, cols)

def gather(shard, count):
    return assemble(gather_xy(gather_z(shard, count), count), count)

def take(value, index, axis):
    return lax.dynamic_index_in_dim(value, index, axis, keepdims=False)

def scatter_core(parts, count):
    me = lax.axis_index(AXES)
    core = me % 2
    planes = count // 8
    split = [p.reshape(planes, 4, 2, p.shape[0] // count, p.shape[1]) for p in parts]
    send = jnp.concatenate([take(p, 1 - core, 2) for p in split], axis=-1)
    keep = jnp.concatenate([take(p, core, 2) for p in split], axis=-1)
    got = shuffle(send, count, lambda d: d ^ 1)
    return (keep.astype(jnp.float32) + got.astype(jnp.float32)).astype(jnp.bfloat16)

def scatter_xy(held, count):
    planes = held.shape[0]
    half = planes // 2
    spot = (lax.axis_index(AXES) // 2) % 4
    f = jnp.float32
    far = take(held, spot ^ 3, 1)
    got_a = shuffle(far[:half], count, lambda d: d ^ 2)
    got_b = shuffle(far[half:], count, lambda d: d ^ 4)
    to_y = take(held, spot ^ 2, 1)
    to_y = jnp.concatenate([(to_y[:half].astype(f) + got_a.astype(f)).astype(jnp.bfloat16), to_y[half:]], axis=0)
    to_x = take(held, spot ^ 1, 1)
    to_x = jnp.concatenate([to_x[:half], (to_x[half:].astype(f) + got_b.astype(f)).astype(jnp.bfloat16)], axis=0)
    from_x = shuffle(to_x, count, lambda d: d ^ 2)
    from_y = shuffle(to_y, count, lambda d: d ^ 4)
    mine = take(held, spot, 1)
    return mine.astype(f) + from_x.astype(f) + from_y.astype(f)

def scatter_z(column, count):
    me = lax.axis_index(AXES)
    total = column
    stride = count
    for radix in digits(count // 8)[::-1]:
        stride //= radix
        mine = (me // stride) % radix
        split = total.reshape((radix, -1) + column.shape[1:])
        low = split.astype(jnp.bfloat16)
        total = take(split, mine, 0)
        for s in range(1, radix):
            item = take(low, (mine + s) % radix, 0)
            came = shuffle(item, count, lambda d, s=s: shifted(d, stride, radix, s))
            total = total + came.astype(jnp.float32)
    return total[0]


def scatter(parts, count):
    return scatter_z(scatter_xy(scatter_core(parts, count), count), count)


def layer_norm(inputs, norm_gain, norm_shift):
    average = jnp.mean(inputs, axis=-1, keepdims=True)
    centered = inputs - average
    spread = jnp.mean(centered * centered, axis=-1, keepdims=True)
    return centered * lax.rsqrt(spread + 1e-06) * norm_gain + norm_shift


def contract_rows(left, right):
    return lax.dot_general(
        left, right, (((0,), (0,)), ((), ())), preferred_element_type=jnp.float32
    )


def contract_cols(left, right):
    return lax.dot_general(
        left, right, (((1,), (1,)), ((), ())), preferred_element_type=jnp.float32
    )


def column_sum(values):
    return jnp.sum(values.astype(jnp.float32), axis=0)


def per_device(
    patches,
    counts,
    cotangent,
    input_weight,
    output_weight,
    expand_weight,
    reduce_weight,
    norm1_gain,
    norm1_shift,
    query_bias,
    value_bias,
    output_bias,
    branch1_scale,
    norm2_gain,
    norm2_shift,
    expand_bias,
    reduce_bias,
    branch2_scale,
):
    count = lax.axis_size("wide") * lax.axis_size("narrow")
    vectors = (
        norm1_gain,
        norm1_shift,
        query_bias,
        value_bias,
        output_bias,
        branch1_scale,
        norm2_gain,
        norm2_shift,
        reduce_bias,
        branch2_scale,
    )
    shard_rows = input_weight.shape[0]
    fold = expand_bias.shape[0] // shard_rows
    side = jnp.concatenate(
        [jnp.stack(vectors, axis=1), expand_bias.reshape(shard_rows, fold)], axis=1
    )
    side = jnp.pad(side, ((0, 0), (0, LANES - side.shape[1])))
    first = gather(jnp.concatenate([input_weight, side], axis=1), count)
    second = gather(jnp.concatenate([output_weight, expand_weight], axis=1), count)
    w_reduce = gather(reduce_weight, count)
    columns = input_weight.shape[1]
    w_input = first[:, :columns]
    w_output = second[:, : output_weight.shape[1]]
    w_expand = second[:, output_weight.shape[1] :]
    side_all = first[:, columns:].astype(jnp.float32)
    (
        gain_one,
        shift_one,
        bias_query,
        bias_value,
        bias_output,
        scale_one,
        gain_two,
        shift_two,
        bias_reduce,
        scale_two,
    ) = tuple(side_all[:, t] for t in range(len(vectors)))
    bias_expand = side_all[:, len(vectors) : len(vectors) + fold].reshape(-1)
    n_images, n_patch, width = patches.shape
    n_rows = n_images * n_patch
    head_shape = (n_images, n_patch, HEADS, HEAD)
    score_scale = HEAD ** (-0.5)
    position = jnp.arange(n_patch, dtype=jnp.int32)
    valid_keys = position[None, :] < counts[:, None]
    row_mask = jnp.where(valid_keys, 1.0, 0.0).astype(jnp.float32).reshape(n_rows, 1)
    rows_in = patches.astype(jnp.float32).reshape(n_rows, width)
    normed_low = layer_norm(rows_in, gain_one, shift_one).astype(jnp.bfloat16)
    projections = jnp.dot(normed_low, w_input, preferred_element_type=jnp.float32)
    queries = (projections[:, :width] + bias_query).astype(jnp.bfloat16).reshape(head_shape)
    key_rows = projections[:, width : 2 * width].astype(jnp.bfloat16).reshape(head_shape)
    values = (projections[:, 2 * width :] + bias_value).astype(jnp.bfloat16).reshape(head_shape)

    def attention_scores():
        raw_scores = jnp.einsum(
            "iphd,iqhd->ihpq", queries, key_rows, preferred_element_type=jnp.float32
        )
        return jnp.where(valid_keys[:, None, None, :], raw_scores * score_scale, -1e30)

    scores = attention_scores()
    log_total = jax.nn.logsumexp(scores, axis=-1, keepdims=True)
    soft_low = jnp.exp(scores - log_total).astype(jnp.bfloat16)
    attended = jnp.einsum("ihpq,iqhd->iphd", soft_low, values, preferred_element_type=jnp.float32)
    attended_low = attended.astype(jnp.bfloat16).reshape(n_rows, width)
    projected = jnp.dot(attended_low, w_output, preferred_element_type=jnp.float32) + bias_output
    middle = rows_in + scale_one * projected
    second_low = layer_norm(middle, gain_two, shift_two).astype(jnp.bfloat16)
    hidden = jnp.dot(second_low, w_expand, preferred_element_type=jnp.float32) + bias_expand
    activated_low = jax.nn.gelu(hidden, approximate=False).astype(jnp.bfloat16)
    branch = jnp.dot(activated_low, w_reduce, preferred_element_type=jnp.float32) + bias_reduce
    outputs = middle + scale_two * branch
    back_input, back_output, back_expand, back_reduce = (w_input, w_output, w_expand, w_reduce)
    grad_out = cotangent.astype(jnp.float32).reshape(n_rows, width) * row_mask
    grad_branch = (grad_out * scale_two).astype(jnp.bfloat16)
    grad_scale_two = jnp.sum(grad_out * branch, axis=0)
    grad_bias_reduce = column_sum(grad_branch)
    grad_w_reduce = contract_rows(activated_low, grad_branch)
    grad_activated = contract_cols(grad_branch, back_reduce)
    gelu_exact = partial(jax.nn.gelu, approximate=False)
    _, gelu_back = jax.vjp(gelu_exact, hidden)
    grad_hidden = gelu_back(grad_activated)[0].astype(jnp.bfloat16)
    grad_bias_expand = column_sum(grad_hidden)
    grad_w_expand = contract_rows(second_low, grad_hidden)
    grad_second = contract_cols(grad_hidden, back_expand)
    _, norm_back_two = jax.vjp(layer_norm, middle, gain_two, shift_two)
    grad_middle, grad_gain_two, grad_shift_two = norm_back_two(grad_second)
    grad_middle = grad_middle + grad_out
    grad_projected = (grad_middle * scale_one).astype(jnp.bfloat16)
    grad_scale_one = jnp.sum(grad_middle * projected, axis=0)
    grad_bias_output = column_sum(grad_projected)
    grad_w_output = contract_rows(attended_low, grad_projected)
    grad_attended = (
        contract_cols(grad_projected, back_output).astype(jnp.bfloat16).reshape(head_shape)
    )
    scores = attention_scores()
    soft_full = jnp.exp(scores - log_total)
    soft_again = soft_full.astype(jnp.bfloat16)
    grad_soft = jnp.einsum(
        "iphd,iqhd->ihpq", grad_attended, values, preferred_element_type=jnp.float32
    )
    grad_values = jnp.einsum(
        "ihpq,iphd->iqhd", soft_again, grad_attended, preferred_element_type=jnp.float32
    ).astype(jnp.bfloat16)
    grad_scores = (
        soft_full * (grad_soft - jnp.sum(soft_full * grad_soft, axis=-1, keepdims=True))
    ).astype(jnp.bfloat16)
    grad_queries = (
        (
            jnp.einsum("ihpq,iqhd->iphd", grad_scores, key_rows, preferred_element_type=jnp.float32)
            * score_scale
        )
        .astype(jnp.bfloat16)
        .reshape(n_rows, width)
    )
    grad_keys = (
        (
            jnp.einsum("ihpq,iphd->iqhd", grad_scores, queries, preferred_element_type=jnp.float32)
            * score_scale
        )
        .astype(jnp.bfloat16)
        .reshape(n_rows, width)
    )
    grad_values = grad_values.reshape(n_rows, width)
    grad_bias_query = column_sum(grad_queries)
    grad_bias_value = column_sum(grad_values)
    grad_projections = jnp.concatenate([grad_queries, grad_keys, grad_values], axis=1)
    grad_w_input = contract_rows(normed_low, grad_projections)
    grad_normed = contract_cols(grad_projections, back_input)
    _, norm_back_one = jax.vjp(layer_norm, rows_in, gain_one, shift_one)
    grad_rows, grad_gain_one, grad_shift_one = norm_back_one(grad_normed)
    input_grad = grad_rows + grad_middle
    grads = (
        grad_gain_one,
        grad_shift_one,
        grad_bias_query,
        grad_bias_value,
        grad_bias_output,
        grad_scale_one,
        grad_gain_two,
        grad_shift_two,
        grad_bias_reduce,
        grad_scale_two,
    )
    side_grad = jnp.concatenate(
        [jnp.stack(grads, axis=1), grad_bias_expand.reshape(width, fold)], axis=1
    )
    side_grad = jnp.pad(side_grad, ((0, 0), (0, LANES - side_grad.shape[1])))
    low = jnp.bfloat16
    sum_reduce = scatter([grad_w_reduce.astype(low)], count)
    sum_second = scatter([grad_w_output.astype(low), grad_w_expand.astype(low)], count)
    sum_first = scatter([grad_w_input.astype(low), side_grad.astype(low)], count)
    sums = tuple(sum_first[:, columns + t] for t in range(len(grads)))
    sum_bias_expand = sum_first[:, columns + len(grads) : columns + len(grads) + fold].reshape(-1)
    return (
        outputs.reshape(n_images, n_patch, width).astype(jnp.bfloat16),
        input_grad.reshape(n_images, n_patch, width),
        sum_first[:, :columns],
        sum_second[:, :width],
        sum_second[:, width:],
        sum_reduce,
        *sums[:8],
        sum_bias_expand,
        *sums[8:],
    )


def solution(mesh):
    placed = (
        P(("wide", "narrow"), None, None),
        P(("wide", "narrow")),
        P(("wide", "narrow"), None, None),
        P(("wide", "narrow"), None),
        P(("wide", "narrow"), None),
        P(("wide", "narrow"), None),
        P(("wide", "narrow"), None),
        P(("wide", "narrow")),
        P(("wide", "narrow")),
        P(("wide", "narrow")),
        P(("wide", "narrow")),
        P(("wide", "narrow")),
        P(("wide", "narrow")),
        P(("wide", "narrow")),
        P(("wide", "narrow")),
        P(("wide", "narrow")),
        P(("wide", "narrow")),
        P(("wide", "narrow")),
    )
    return jax.shard_map(
        per_device,
        mesh=mesh,
        in_specs=placed,
        out_specs=(
            P(("wide", "narrow"), None, None),
            P(("wide", "narrow"), None, None),
            P(("wide", "narrow"), None),
            P(("wide", "narrow"), None),
            P(("wide", "narrow"), None),
            P(("wide", "narrow"), None),
            P(("wide", "narrow")),
            P(("wide", "narrow")),
            P(("wide", "narrow")),
            P(("wide", "narrow")),
            P(("wide", "narrow")),
            P(("wide", "narrow")),
            P(("wide", "narrow")),
            P(("wide", "narrow")),
            P(("wide", "narrow")),
            P(("wide", "narrow")),
            P(("wide", "narrow")),
        ),
        check_vma=False,
    )
```

time: 798 us -> 444 us (0.56)
  waiting for transfers between devices: 356 us -> 83.2 us
  blocking collectives: 91.1 us -> 0 us
  starting transfers between devices: 0.48 us -> 52.3 us
  other arithmetic: 76 us -> 41.8 us
  local copies, waits for them, and re-layouts: 86.7 us -> 116 us
  between operations: 17.9 us -> 2.32 us
  matrix products: 165 us -> 150 us
    reduce_scatter x8 -> x0, waiting for transfers between devices: 253 us -> none  [the longest x1 72.8 us: per_device(): lax.psum_scatter(inner[3], 'wide', scatter_dimension=0, tiled=True)]
    all_gather x4 -> x0, waiting for transfers between devices: 99.5 us -> none  [the longest x1 58.6 us: per_device(): lax.all_gather(expand_weight, ('wide', 'narrow'), axis=0, tiled=True)]
    unnamed x3 -> x0, blocking collectives: 91.1 us -> none
    ppermute x0 -> x48, waiting for transfers between devices: none -> 83.2 us  [shuffle(): return lax.ppermute(value, AXES, [(d, target(d)) for d in range(count)])]
    ppermute x0 -> x48, starting transfers between devices: none -> 52.3 us  [shuffle(): return lax.ppermute(value, AXES, [(d, target(d)) for d in range(count)])]
    convert_element_type x23 -> x10, other arithmetic: 42.8 us -> 5.9 us  [the longest x3 3.41 us: scatter_z(): low = split.astype(jnp.bfloat16)]
    dynamic_update_slice x0 -> x32, local copies, waits for them, and re-layouts: none -> 27.7 us  [the longest x15 9.52 us: put(): return lax.dynamic_update_slice(buf, item[:, None], (z, yx, 0, 0))]
    convert_element_type x38 -> x0, local copies, waits for them, and re-layouts: 19.2 us -> none  [the longest x1 8.95 us: per_device(): activated_low = jax.nn.gelu(hidden, approximate=False).astype(jnp.bfloat16)]
  transfers between devices with their start and end apart: 12 -> 48, of which waited for: 8 -> 18; matrix products, arithmetic and copies ran while one was open for 37% -> 30% of each run, Pallas kernels for 0% -> 0%
where the time goes in v1:
time: 444 us; the launch traced here: 445 us
  matrix products  150 us (34%)
  local copies, waits for them, and re-layouts  116 us (26%)
  waiting for transfers between devices  83.2 us (19%)
  starting transfers between devices  52.3 us (12%)
  other arithmetic  41.8 us (9%)
    ppermute x48, waiting for transfers between devices, shuffle(): return lax.ppermute(value, AXES, [(d, target(d)) for d in range(count)])  83.2 us
    ppermute x48, starting transfers between devices, shuffle(): return lax.ppermute(value, AXES, [(d, target(d)) for d in range(count)])  52.3 us
    dot_general x1, matrix products, per_device(): jnp.dot(second_low, w_expand, preferred_element_type=jnp.float32)  35.4 us
    dot_general x4, matrix products, contract_cols(): lax.dot_general(left, right, (((1,), (1,)), ((), ())), preferred_element_...  35.1 us
    dot_general x4, matrix products, contract_rows(): lax.dot_general(left, right, (((0,), (0,)), ((), ())), preferred_element_...  25.8 us
    convert_element_type x1, local copies, waits for them, and re-layouts, per_device(): (projections[:, :width] + bias_query).astype(jnp.bfloat16)  12.2 us
    unnamed x146, local copies, waits for them, and re-layouts  10.5 us
    dot_general x1, matrix products, per_device(): jnp.dot(activated_low, w_reduce, preferred_element_type=jnp.float32)  10.3 us
  transfers between devices with their start and end apart: 48, of which 18 were waited for; matrix products, arithmetic and copies ran while one was open for 30% of the time, Pallas kernels for 0%

profile of v1, /device:TPU:0, one launch (start us, length us, event | category | flops | bytes accessed | tf_op | source)
XLA Modules:
  0.0 445.4 jit_solution(530493640591123117)
XLA Ops:
  0.7 3.1 collective-permute-start.16
  3.8 2.6 collective-permute-start.17
  33.0 3.6 collective-permute-start.10
  50.0 3.7 collective-permute-done.4
  56.0 10.4 %collective-permute-done.20 = bf16[4,96,768]{2,1,0:T(8,128)(2,1)S(1)} collective-permute-done((bf16[4,96,768]{2,1,0:T(8,128)(2,1)S(1)}, bf16[4,96,768]{2,1,0:T(8,128)(2,1)S(1)}, u32[]{:S(2)}, u32[]{:S(2)}) %collective-permute-start.20) | collective-permute-done | bytes 589856 | tf_op jit(solution)/shard_map/ppermute | solution.py:15
  70.3 14.6 %collective-permute-done.5 = bf16[2,24,2432]{2,1,0:T(8,128)(2,1)S(1)} collective-permute-done((bf16[2,24,2432]{2,1,0:T(8,128)(2,1)S(1)}, bf16[2,24,2432]{2,1,0:T(8,128)(2,1)S(1)}, u32[]{:S(2)}, u32[]{:S(2)}) %collective-permute-start.5) | collective-permute-done | bytes 233504 | tf_op jit(solution)/shard_map/ppermute | solution.py:15
  95.1 3.1 collective-permute-done.13
  100.7 2.2 bitcast_dynamic-update-slice_fusion
  103.3 3.0 slice_reduce_fusion.3
  107.0 3.9 fusion.28
  114.0 12.2 %copy.305 = bf16[1024,768]{0,1:T(8,128)(2,1)} copy(bf16[1024,768]{1,0:T(8,128)(2,1)S(1)} %get-tuple-element.62) | data formatting | bytes 3145728 | tf_op jit(solution)/shard_map/convert_element_type | solution.py:226
  126.2 2.9 reshape.360
  129.1 3.2 copy.306
  132.2 3.9 reshape.361
  136.1 9.4 %fusion.6 = (f32[4,12,256]{2,1,0:T(8,128)}, f32[4,12,256,256]{2,3,1,0:T(8,128)}) fusion(pred[4,256]{1,0:T(4,128)(4,1)S(1)} %iota_compare_fusion.1, bf16[4,256,12,64]{1,0,3,2:T(4,128)(2,1)} %reshape.361, bf16[4,256,12,64]{1,0,3,2:T(4,128)(2,1)S(1)} %reshape.360), kind=kOutput, calls=%fused_computation.22 | convolution fusion | flops 412078080 | bytes 15778816 | tf_op jit(solution)/shard_map/iphd,iqhd->ihpq/dot_general | solution.py:231
  146.5 2.7 copy.304
  149.2 2.9 reshape.359
  152.1 8.5 %exponential_reduce_fusion = f32[4,12,256]{2,1,0:T(8,128)S(1)} fusion(f32[4,12,256,256]{2,3,1,0:T(8,128)} %get-tuple-element.109, f32[4,12,256]{2,1,0:T(8,128)S(1)} %is-finite_select_fusion, pred[4,256]{1,0:T(4,128)(4,1)S(1)} %iota_compare_fusion.1), kind=kLoop, calls=%fused_computation.19 | loop fusion | flops 12570624 | bytes 12682240 | tf_op jit(solution)/shard_map/reduce_sum | solution.py:237
  160.8 3.0 fusion.30
  167.4 2.4 fusion.76
  170.6 3.2 bitcast_dynamic-update-slice_fusion.3
  173.9 3.7 bitcast_dynamic-update-slice_fusion.1
  177.6 4.8 %fusion.80 = (f32[1024]{0:T(1024)S(1)}, f32[1024,768]{1,0:T(8,128)S(1)}, f32[1024,768]{1,0:T(8,128)}) fusion(f32[768]{0:T(1024)S(1)} %copy-done.50, f32[768]{0:T(1024)S(1)} %get-tuple-element.35, bf16[4,256,768]{2,1,0:T(8,128)(2,1)S(1)} %copy-done.1, bf16[1024,768]{0,1:T(8,128)(2,1)S(1)} %bitcast.361, bf16[768,3840]{1,0:T(8,128)(2,1)} %bitcast.346), kind=kOutput, calls=%fused_computation.261 | convolution fusion | flops 1211890688 | bytes 10627072 | tf_op jit(solution)/shard_map/dot_general | solution.py:241
  183.1 35.4 %multiply_convert_fusion.1 = (bf16[1024,3072]{1,0:T(8,128)(2,1)}, f32[1024,3072]{1,0:T(8,128)}, f32[1024,3072]{1,0:T(8,128)}) fusion(f32[3072]{0:T(1024)S(1)} %copy-done.52, bf16[768,3840]{1,0:T(8,128)(2,1)S(1)} %bitcast.351, f32[1024,768]{1,0:T(8,128)S(1)} %get-tuple-element.61, f32[768]{0:T(1024)S(1)} %copy-done.55, f32[768]{0:T(1024)S(1)} %get-tuple-element.29, ...), kind=kOutput, calls=%fused_computation.5 | convolution fusion | flops 5043388416 | bytes 39350272 | tf_op jit(solution)/shard_map/dot_general | solution.py:244
  218.6 17.4 %fusion.83 = (bf16[3072]{0:T(1024)(128)(2,1)}, bf16[1024,3072]{1,0:T(8,128)(2,1)}) fusion(f32[1024,3072]{1,0:T(8,128)} %get-tuple-element.59, bf16[1024,768]{1,0:T(8,128)(2,1)S(1)} %bitcast.384, bf16[3072,768]{1,0:T(8,128)(2,1)} %bitcast.367, f32[1024,3072]{1,0:T(8,128)} %get-tuple-element.111, f32[3072]{0:T(1024)S(1)} %copy-done.52), kind=kOutput, calls=%fused_computation.264 | convolution fusion | flops 4882166784 | bytes 37767168 | tf_op jit(solution)/shard_map/dot_general | solution.py:147
  235.9 9.9 %multiply_reduce_fusion.2 = (bf16[768]{0:T(1024)(128)(2,1)}, f32[1024]{0:T(1024)S(1)}, bf16[768]{0:T(1024)(128)(2,1)}, f32[1024,768]{1,0:T(8,128)S(1)}) fusion(f32[1024,768]{1,0:T(8,128)S(1)} %get-tuple-element.61, f32[1024]{0:T(1024)S(1)} %fusion.61, f32[1024]{0:T(1024)S(1)} %broadcast_multiply_fusion, f32[768]{0:T(1024)S(1)} %get-tuple-element.29, ...), kind=kOutput, calls=%fused_computation.60 | convolution fusion | flops 4838126592 | bytes 17319936 | tf_op jit(solution)/shard_map/dot_general | solution.py:147
  250.9 2.7 convolution_convert_fusion.5
  255.6 8.5 %fusion.82 = (bf16[12,64]{1,0:T(8,128)(2,1)}, bf16[4,256,12,64]{1,3,2,0:T(8,128)(2,1)S(1)}) fusion(f32[4,12,256,256]{2,3,1,0:T(8,128)} %get-tuple-element.109, f32[4,12,256]{2,1,0:T(8,128)S(1)} %copy-done.30, pred[4,256]{1,0:T(4,128)(4,1)S(1)} %iota_compare_fusion.1, bf16[4,256,12,64]{1,0,3,2:T(4,128)(2,1)S(1)} %reshape.368), kind=kOutput, calls=%fused_computation.263 | convolution fusion | flops 416808192 | bytes 15780352 | tf_op jit(solution)/shard_map/ihpq,iphd->iqhd/dot_general | solution.py:277
  264.1 10.2 %multiply_reduce_fusion = (f32[4,12,256]{2,1,0:T(8,128)S(1)}, f32[4,12,256,256]{2,3,1,0:T(8,128)}) fusion(f32[4,12,256,256]{2,3,1,0:T(8,128)} %get-tuple-element.109, f32[4,12,256]{2,1,0:T(8,128)S(1)} %copy-done.30, pred[4,256]{1,0:T(4,128)(4,1)S(1)} %iota_compare_fusion.1, bf16[4,256,12,64]{1,0,3,2:T(4,128)(2,1)S(1)} %copy-done.11, ...), kind=kOutput, calls=%fused_computation.3 | convolution fusion | flops 418369536 | bytes 28410880 | tf_op jit(solution)/shard_map/iphd,iqhd->ihpq/dot_general | solution.py:274
  274.3 8.2 %multiply_convert_fusion = bf16[4,12,256,256]{2,3,1,0:T(8,128)(2,1)S(1)} fusion(f32[4,12,256,256]{2,3,1,0:T(8,128)} %get-tuple-element.114, f32[4,12,256,256]{2,3,1,0:T(8,128)S(1)} %bitcast.343, f32[4,12,256]{2,1,0:T(8,128)S(1)} %get-tuple-element.113, f32[4,12,256]{2,1,0:T(8,128)S(1)} %copy-done.30, pred[4,256]{1,0:T(4,128)(4,1)S(1)} %iota_compare_fusion.1), kind=kLoop, calls=%fused_computation.2 | loop fusion | flops 18874368 | bytes 31556608 | tf_op jit(solution)/shard_map/convert_element_type | solution.py:282
  293.3 5.1 %fusion.69 = (bf16[768]{0:T(1024)(128)(2,1)S(1)}, f32[1024]{0:T(1024)S(1)}, f32[1024,768]{1,0:T(8,128)S(1)}) fusion(f32[768]{0:T(1024)S(1)} %copy-done.41, f32[1024]{0:T(1024)S(1)} %bitcast.394, bf16[4,256,768]{2,1,0:T(8,128)(2,1)S(1)} %copy-done.2, bf16[1024,2304]{0,1:T(8,128)(2,1)S(1)} %constant_dynamic-update-slice_fusion.2, ...), kind=kOutput, calls=%fused_computation.254 | convolution fusion | flops 3628595456 | bytes 12989952 | tf_op jit(solution)/shard_map/dot_general | solution.py:147
  298.4 5.5 %convolution_convert_fusion.2 = bf16[768,2304]{1,0:T(8,128)(2,1)} fusion(bf16[1024,768]{1,0:T(8,128)(2,1)S(1)} %copy-done.24, bf16[1024,2304]{0,1:T(8,128)(2,1)S(1)} %constant_dynamic-update-slice_fusion.2), kind=kOutput, calls=%fused_computation.27 | convolution fusion | flops 3625648128 | bytes 9830400 | tf_op jit(solution)/shard_map/dot_general | solution.py:141
  306.3 10.3 %multiply_reduce_fusion.1 = (bf16[768]{0:T(1024)(128)(2,1)S(1)}, bf16[768]{0:T(1024)(128)(2,1)S(1)}, f32[1024,768]{1,0:T(8,128)}, bf16[1024,768]{1,0:T(8,128)(2,1)}, bf16[1024,768]{1,0:T(8,128)(2,1)S(1)}) fusion(bf16[4,256,768]{2,1,0:T(8,128)(2,1)S(1)} %copy-done.15, f32[1024]{0:T(1024)S(1)} %bitcast.400, f32[768]{0:T(1024)S(1)} %copy-done.57, ...), kind=kOutput, calls=%fused_computation.59 | convolution fusion | flops 4850710528 | bytes 33070080 | tf_op jit(solution)/shard_map/dot_general | solution.py:246
  316.7 9.8 %convolution_convert_fusion = bf16[3072,768]{1,0:T(8,128)(2,1)} fusion(bf16[1024,3072]{1,0:T(8,128)(2,1)} %get-tuple-element.58, bf16[1024,768]{1,0:T(8,128)(2,1)S(1)} %get-tuple-element.90), kind=kOutput, calls=%fused_computation.25 | convolution fusion | flops 4834197504 | bytes 12582912 | tf_op jit(solution)/shard_map/dot_general | solution.py:141
  337.0 3.3 concatenate.50
  341.4 2.3 constant_dynamic-slice_fusion.16
  344.5 9.1 %convolution_convert_fusion.1 = bf16[768,3072]{1,0:T(8,128)(2,1)S(1)} fusion(bf16[1024,3072]{1,0:T(8,128)(2,1)} %get-tuple-element.121, f32[1024,768]{1,0:T(8,128)S(1)} %copy-done.4, f32[768]{0:T(1024)S(1)} %copy-done.56, f32[768]{0:T(1024)S(1)} %copy-done.48, f32[1024]{0:T(1024)S(1)} %copy-done.44, f32[1024]{0:T(1024)S(1)} %broadcast_multiply_fusion), kind=kOutput, calls=%fused_computation.26 | convolution fusion | flops 4838129664 | bytes 14170112 | tf_op jit(solution)/shard_map/dot_general | solution.py:141
  362.7 4.4 collective-permute-done.25
  373.7 8.4 %collective-permute-done.26 = bf16[4,24,2432]{2,1,0:T(8,128)(2,1)S(1)} collective-permute-done((bf16[4,24,2432]{2,1,0:T(8,128)(2,1)S(1)}, bf16[4,24,2432]{2,1,0:T(8,128)(2,1)S(1)}, u32[]{:S(2)}, u32[]{:S(2)}) %collective-permute-start.26) | collective-permute-done | bytes 466976 | tf_op jit(solution)/shard_map/ppermute | solution.py:15
  386.1 2.8 collective-permute-start.31
  392.9 6.2 %collective-permute-done.33 = bf16[2,24,3840]{2,1,0:T(8,128)(2,1)S(1)} collective-permute-done((bf16[2,24,3840]{2,1,0:T(8,128)(2,1)S(1)}, bf16[2,24,3840]{2,1,0:T(8,128)(2,1)S(1)}, u32[]{:S(2)}, u32[]{:S(2)}) %collective-permute-start.33) | collective-permute-done | bytes 368672 | tf_op jit(solution)/shard_map/ppermute | solution.py:15
  400.4 2.4 collective-permute-start.44
  407.7 7.9 %collective-permute-done.42 = bf16[4,96,768]{2,1,0:T(8,128)(2,1)} collective-permute-done((bf16[4,96,768]{2,1,0:T(8,128)(2,1)}, bf16[4,96,768]{2,1,0:T(8,128)(2,1)}, u32[]{:S(2)}, u32[]{:S(2)}) %collective-permute-start.42) | collective-permute-done | bytes 589856 | tf_op jit(solution)/shard_map/ppermute | solution.py:15
  419.1 3.7 collective-permute-start.47
  422.9 3.6 collective-permute-done.34
  429.3 2.8 collective-permute-start.39
  432.9 4.3 collective-permute-done.37
  437.2 6.6 %collective-permute-done.38 = bf16[1,24,3840]{2,1,0:T(8,128)(2,1)S(1)} collective-permute-done((bf16[1,24,3840]{2,1,0:T(8,128)(2,1)S(1)}, bf16[1,24,3840]{2,1,0:T(8,128)(2,1)S(1)}, u32[]{:S(2)}, u32[]{:S(2)}) %collective-permute-start.38) | collective-permute-done | bytes 184352 | tf_op jit(solution)/shard_map/ppermute | solution.py:15
  (377 shorter events, 139.2 us)
Async XLA Ops:
  0.7 32.3 %collective-permute-start.16 = (bf16[1,96,768]{2,1,0:T(8,128)(2,1)}, bf16[1,96,768]{2,1,0:T(8,128)(2,1)}, u32[]{:S(2)}, u32[]{:S(2)}) collective-permute-start(bf16[1,96,768]{2,1,0:T(8,128)(2,1)} %bitcast.390), channel_id=1, source_target_pairs={{0,8},{1,9},{2,10},{3,11},{4,12},{5,13},{6,14},{7,15},{8,16},{9,17... | collective-permute-start | bytes 442376 | tf_op jit(solution)/shard_map/ppermute | solution.py:15
  3.8 33.8 %collective-permute-start.17 = (bf16[1,96,768]{2,1,0:T(8,128)(2,1)}, bf16[1,96,768]{2,1,0:T(8,128)(2,1)}, u32[]{:S(2)}, u32[]{:S(2)}) collective-permute-start(bf16[1,96,768]{2,1,0:T(8,128)(2,1)} %bitcast.391), channel_id=1, source_target_pairs={{0,16},{1,17},{2,18},{3,19},{4,20},{5,21},{6,22},{7,23},{8,24},{9,... | collective-permute-start | bytes 442376 | tf_op jit(solution)/shard_map/ppermute | solution.py:15
  6.4 33.7 %collective-permute-start.18 = (bf16[1,96,768]{2,1,0:T(8,128)(2,1)}, bf16[1,96,768]{2,1,0:T(8,128)(2,1)S(1)}, u32[]{:S(2)}, u32[]{:S(2)}) collective-permute-start(bf16[1,96,768]{2,1,0:T(8,128)(2,1)} %bitcast.392), channel_id=1, source_target_pairs={{0,24},{1,25},{2,26},{3,27},{4,28},{5,29},{6,30},{7,31},{8,0},{9,1... | collective-permute-start | bytes 442376 | tf_op jit(solution)/shard_map/ppermute | solution.py:15
  17.6 7.6 %collective-permute-start = (bf16[1,24,2432]{2,1,0:T(8,128)(2,1)}, bf16[1,24,2432]{2,1,0:T(8,128)(2,1)}, u32[]{:S(2)}, u32[]{:S(2)}) collective-permute-start(bf16[1,24,2432]{2,1,0:T(8,128)(2,1)} %fusion.60), channel_id=1, source_target_pairs={{0,8},{1,9},{2,10},{3,11},{4,12},{5,13},{6,14},{7,15},{8,16},{9,17... | collective-permute-start | bytes 350216 | tf_op jit(solution)/shard_map/ppermute | solution.py:15
  18.3 10.7 %collective-permute-start.1 = (bf16[1,24,2432]{2,1,0:T(8,128)(2,1)}, bf16[1,24,2432]{2,1,0:T(8,128)(2,1)}, u32[]{:S(2)}, u32[]{:S(2)}) collective-permute-start(bf16[1,24,2432]{2,1,0:T(8,128)(2,1)} %fusion.60), channel_id=1, source_target_pairs={{0,16},{1,17},{2,18},{3,19},{4,20},{5,21},{6,22},{7,23},{8,24},{9,... | collective-permute-start | bytes 350216 | tf_op jit(solution)/shard_map/ppermute | solution.py:15
  25.2 5.4 %collective-permute-start.2 = (bf16[1,24,2432]{2,1,0:T(8,128)(2,1)}, bf16[1,24,2432]{2,1,0:T(8,128)(2,1)S(1)}, u32[]{:S(2)}, u32[]{:S(2)}) collective-permute-start(bf16[1,24,2432]{2,1,0:T(8,128)(2,1)} %fusion.60), channel_id=1, source_target_pairs={{0,24},{1,25},{2,26},{3,27},{4,28},{5,29},{6,30},{7,31},{8,0},{9,1... | collective-permute-start | bytes 350216 | tf_op jit(solution)/shard_map/ppermute | solution.py:15
  29.0 15.2 %collective-permute-start.8 = (bf16[1,24,3840]{2,1,0:T(8,128)(2,1)S(1)}, bf16[1,24,3840]{2,1,0:T(8,128)(2,1)S(1)}, u32[]{:S(2)}, u32[]{:S(2)}) collective-permute-start(bf16[1,24,3840]{2,1,0:T(8,128)(2,1)S(1)} %bitcast.387), channel_id=1, source_target_pairs={{0,8},{1,9},{2,10},{3,11},{4,12},{5,13},{6,14},{7,15},{8,16},{9,17... | collective-permute-start | bytes 552968 | tf_op jit(solution)/shard_map/ppermute | solution.py:15
  30.5 14.2 %collective-permute-start.9 = (bf16[1,24,3840]{2,1,0:T(8,128)(2,1)S(1)}, bf16[1,24,3840]{2,1,0:T(8,128)(2,1)S(1)}, u32[]{:S(2)}, u32[]{:S(2)}) collective-permute-start(bf16[1,24,3840]{2,1,0:T(8,128)(2,1)S(1)} %bitcast.388), channel_id=1, source_target_pairs={{0,16},{1,17},{2,18},{3,19},{4,20},{5,21},{6,22},{7,23},{8,24},{9,... | collective-permute-start | bytes 552968 | tf_op jit(solution)/shard_map/ppermute | solution.py:15
  33.0 12.7 %collective-permute-start.10 = (bf16[1,24,3840]{2,1,0:T(8,128)(2,1)S(1)}, bf16[1,24,3840]{2,1,0:T(8,128)(2,1)S(1)}, u32[]{:S(2)}, u32[]{:S(2)}) collective-permute-start(bf16[1,24,3840]{2,1,0:T(8,128)(2,1)S(1)} %bitcast.389), channel_id=1, source_target_pairs={{0,24},{1,25},{2,26},{3,27},{4,28},{5,29},{6,30},{7,31},{8,0},{9,1... | collective-permute-start | bytes 552968 | tf_op jit(solution)/shard_map/ppermute | solution.py:15
  37.6 17.7 %collective-permute-start.3 = (bf16[4,24,2432]{2,1,0:T(8,128)(2,1)}, bf16[4,24,2432]{2,1,0:T(8,128)(2,1)S(1)}, u32[]{:S(2)}, u32[]{:S(2)}) collective-permute-start(bf16[4,24,2432]{2,1,0:T(8,128)(2,1)} %bitcast.382), channel_id=1, source_target_pairs={{0,2},{1,3},{2,0},{3,1},{4,6},{5,7},{6,4},{7,5},{8,10},{9,11},{10,... | collective-permute-start | bytes 1400840 | tf_op jit(solution)/shard_map/ppermute | solution.py:15
  40.1 13.6 %collective-permute-start.4 = (bf16[4,24,2432]{2,1,0:T(8,128)(2,1)S(1)}, bf16[4,24,2432]{2,1,0:T(8,128)(2,1)S(1)}, u32[]{:S(2)}, u32[]{:S(2)}) collective-permute-start(bf16[4,24,2432]{2,1,0:T(8,128)(2,1)S(1)} %bitcast.383), channel_id=1, source_target_pairs={{0,4},{1,5},{2,6},{3,7},{4,0},{5,1},{6,2},{7,3},{8,12},{9,13},{10,... | collective-permute-start | bytes 1400840 | tf_op jit(solution)/shard_map/ppermute | solution.py:15
  44.2 23.7 %collective-permute-start.19 = (bf16[4,96,768]{2,1,0:T(8,128)(2,1)S(1)}, bf16[4,96,768]{2,1,0:T(8,128)(2,1)S(1)}, u32[]{:S(2)}, u32[]{:S(2)}) collective-permute-start(bf16[4,96,768]{2,1,0:T(8,128)(2,1)S(1)} %bitcast.380), channel_id=1, source_target_pairs={{0,2},{1,3},{2,0},{3,1},{4,6},{5,7},{6,4},{7,5},{8,10},{9,11},{10,... | collective-permute-start | bytes 1769480 | tf_op jit(solution)/shard_map/ppermute | solution.py:15
  44.8 21.6 %collective-permute-start.20 = (bf16[4,96,768]{2,1,0:T(8,128)(2,1)S(1)}, bf16[4,96,768]{2,1,0:T(8,128)(2,1)S(1)}, u32[]{:S(2)}, u32[]{:S(2)}) collective-permute-start(bf16[4,96,768]{2,1,0:T(8,128)(2,1)S(1)} %bitcast.381), channel_id=1, source_target_pairs={{0,4},{1,5},{2,6},{3,7},{4,0},{5,1},{6,2},{7,3},{8,12},{9,13},{10,... | collective-permute-start | bytes 1769480 | tf_op jit(solution)/shard_map/ppermute | solution.py:15
  48.5 40.2 %collective-permute-start.11 = (bf16[4,24,3840]{2,1,0:T(8,128)(2,1)S(1)}, bf16[4,24,3840]{2,1,0:T(8,128)(2,1)S(1)}, u32[]{:S(2)}, u32[]{:S(2)}) collective-permute-start(bf16[4,24,3840]{2,1,0:T(8,128)(2,1)S(1)} %bitcast.375), channel_id=1, source_target_pairs={{0,2},{1,3},{2,0},{3,1},{4,6},{5,7},{6,4},{7,5},{8,10},{9,11},{10,... | collective-permute-start | bytes 2211848 | tf_op jit(solution)/shard_map/ppermute | solution.py:15
  53.7 33.4 %collective-permute-start.12 = (bf16[4,24,3840]{2,1,0:T(8,128)(2,1)S(1)}, bf16[4,24,3840]{2,1,0:T(8,128)(2,1)S(1)}, u32[]{:S(2)}, u32[]{:S(2)}) collective-permute-start(bf16[4,24,3840]{2,1,0:T(8,128)(2,1)S(1)} %bitcast.376), channel_id=1, source_target_pairs={{0,4},{1,5},{2,6},{3,7},{4,0},{5,1},{6,2},{7,3},{8,12},{9,13},{10,... | collective-permute-start | bytes 2211848 | tf_op jit(solution)/shard_map/ppermute | solution.py:15
  55.3 29.6 %collective-permute-start.5 = (bf16[2,24,2432]{2,1,0:T(8,128)(2,1)S(1)}, bf16[2,24,2432]{2,1,0:T(8,128)(2,1)S(1)}, u32[]{:S(2)}, u32[]{:S(2)}) collective-permute-start(bf16[2,24,2432]{2,1,0:T(8,128)(2,1)S(1)} %slice.279), channel_id=1, source_target_pairs={{0,2},{1,3},{2,0},{3,1},{4,6},{5,7},{6,4},{7,5},{8,10},{9,11},{10,... | collective-permute-start | bytes 700424 | tf_op jit(solution)/shard_map/ppermute | solution.py:15
  66.4 20.1 %collective-permute-start.6 = (bf16[2,24,2432]{2,1,0:T(8,128)(2,1)S(1)}, bf16[2,24,2432]{2,1,0:T(8,128)(2,1)S(1)}, u32[]{:S(2)}, u32[]{:S(2)}) collective-permute-start(bf16[2,24,2432]{2,1,0:T(8,128)(2,1)S(1)} %slice.280), channel_id=1, source_target_pairs={{0,4},{1,5},{2,6},{3,7},{4,0},{5,1},{6,2},{7,3},{8,12},{9,13},{10,... | collective-permute-start | bytes 700424 | tf_op jit(solution)/shard_map/ppermute | solution.py:15
  67.9 23.2 %collective-permute-start.21 = (bf16[2,96,768]{2,1,0:T(8,128)(2,1)S(1)}, bf16[2,96,768]{2,1,0:T(8,128)(2,1)S(1)}, u32[]{:S(2)}, u32[]{:S(2)}) collective-permute-start(bf16[2,96,768]{2,1,0:T(8,128)(2,1)S(1)} %slice.300), channel_id=1, source_target_pairs={{0,2},{1,3},{2,0},{3,1},{4,6},{5,7},{6,4},{7,5},{8,10},{9,11},{10,... | collective-permute-start | bytes 884744 | tf_op jit(solution)/shard_map/ppermute | solution.py:15
  84.9 7.0 %collective-permute-start.22 = (bf16[2,96,768]{2,1,0:T(8,128)(2,1)S(1)}, bf16[2,96,768]{2,1,0:T(8,128)(2,1)S(1)}, u32[]{:S(2)}, u32[]{:S(2)}) collective-permute-start(bf16[2,96,768]{2,1,0:T(8,128)(2,1)S(1)} %slice.301), channel_id=1, source_target_pairs={{0,4},{1,5},{2,6},{3,7},{4,0},{5,1},{6,2},{7,3},{8,12},{9,13},{10,... | collective-permute-start | bytes 884744 | tf_op jit(solution)/shard_map/ppermute | solution.py:15
  86.5 16.5 %collective-permute-start.7 = (bf16[4,4,24,2432]{3,2,1,0:T(8,128)(2,1)S(1)}, bf16[4,4,24,2432]{3,2,1,0:T(8,128)(2,1)S(1)}, u32[]{:S(2)}, u32[]{:S(2)}) collective-permute-start(bf16[4,4,24,2432]{3,2,1,0:T(8,128)(2,1)S(1)} %bitcast_dynamic-update-slice_fusion.20), channel_id=1, source_target_pairs={{0,1},{1,0},{2,3},{3,2},{4,5},{5,4},{6,7},{7,6},{8,9},{9,8},{10,11... | collective-permute-start | bytes 5603336 | tf_op jit(solution)/shard_map/ppermute | solution.py:15
  87.1 11.1 %collective-permute-start.13 = (bf16[2,24,3840]{2,1,0:T(8,128)(2,1)S(1)}, bf16[2,24,3840]{2,1,0:T(8,128)(2,1)S(1)}, u32[]{:S(2)}, u32[]{:S(2)}) collective-permute-start(bf16[2,24,3840]{2,1,0:T(8,128)(2,1)S(1)} %slice.291), channel_id=1, source_target_pairs={{0,2},{1,3},{2,0},{3,1},{4,6},{5,7},{6,4},{7,5},{8,10},{9,11},{10,... | collective-permute-start | bytes 1105928 | tf_op jit(solution)/shard_map/ppermute | solution.py:15
  88.7 10.8 %collective-permute-start.14 = (bf16[2,24,3840]{2,1,0:T(8,128)(2,1)S(1)}, bf16[2,24,3840]{2,1,0:T(8,128)(2,1)S(1)}, u32[]{:S(2)}, u32[]{:S(2)}) collective-permute-start(bf16[2,24,3840]{2,1,0:T(8,128)(2,1)S(1)} %slice.292), channel_id=1, source_target_pairs={{0,4},{1,5},{2,6},{3,7},{4,0},{5,1},{6,2},{7,3},{8,12},{9,13},{10,... | collective-permute-start | bytes 1105928 | tf_op jit(solution)/shard_map/ppermute | solution.py:15
  92.6 78.0 %collective-permute-start.23 = (bf16[4,4,96,768]{3,2,1,0:T(8,128)(2,1)}, bf16[4,4,96,768]{3,2,1,0:T(8,128)(2,1)}, u32[]{:S(2)}, u32[]{:S(2)}) collective-permute-start(bf16[4,4,96,768]{3,2,1,0:T(8,128)(2,1)} %bitcast_dynamic-update-slice_fusion.18), channel_id=1, source_target_pairs={{0,1},{1,0},{2,3},{3,2},{4,5},{5,4},{6,7},{7,6},{8,9},{9,8},{10,11... | collective-permute-start | bytes 7077896 | tf_op jit(solution)/shard_map/ppermute | solution.py:15
  100.3 73.6 %collective-permute-start.15 = (bf16[4,4,24,3840]{3,2,1,0:T(8,128)(2,1)}, bf16[4,4,24,3840]{3,2,1,0:T(8,128)(2,1)}, u32[]{:S(2)}, u32[]{:S(2)}) collective-permute-start(bf16[4,4,24,3840]{3,2,1,0:T(8,128)(2,1)} %bitcast_dynamic-update-slice_fusion.16), channel_id=1, source_target_pairs={{0,1},{1,0},{2,3},{3,2},{4,5},{5,4},{6,7},{7,6},{8,9},{9,8},{10,11... | collective-permute-start | bytes 8847368 | tf_op jit(solution)/shard_map/ppermute | solution.py:15
  343.9 14.5 %collective-permute-start.24 = (bf16[4,4,24,2432]{3,2,0,1:T(8,128)(2,1)S(1)}, bf16[4,4,24,2432]{3,2,0,1:T(8,128)(2,1)S(1)}, u32[]{:S(2)}, u32[]{:S(2)}) collective-permute-start(bf16[4,4,24,2432]{3,2,0,1:T(8,128)(2,1)S(1)} %pad_maximum_fusion.1), channel_id=1, source_target_pairs={{0,1},{1,0},{2,3},{3,2},{4,5},{5,4},{6,7},{7,6},{8,9},{9,8},{10,11... | collective-permute-start | bytes 5603336 | tf_op jit(solution)/shard_map/ppermute | solution.py:15
  354.2 16.4 %collective-permute-start.40 = (bf16[4,4,96,768]{3,2,0,1:T(8,128)(2,1)S(1)}, bf16[4,4,96,768]{3,2,0,1:T(8,128)(2,1)S(1)}, u32[]{:S(2)}, u32[]{:S(2)}) collective-permute-start(bf16[4,4,96,768]{3,2,0,1:T(8,128)(2,1)S(1)} %bitcast.379), channel_id=1, source_target_pairs={{0,1},{1,0},{2,3},{3,2},{4,5},{5,4},{6,7},{7,6},{8,9},{9,8},{10,11... | collective-permute-start | bytes 7077896 | tf_op jit(solution)/shard_map/ppermute | solution.py:15
  359.1 8.0 %collective-permute-start.25 = (bf16[2,24,2432]{2,1,0:T(8,128)(2,1)S(1)}, bf16[2,24,2432]{2,1,0:T(8,128)(2,1)S(1)}, u32[]{:S(2)}, u32[]{:S(2)}) collective-permute-start(bf16[2,24,2432]{2,1,0:T(8,128)(2,1)S(1)} %get-tuple-element.85), channel_id=1, source_target_pairs={{0,4},{1,5},{2,6},{3,7},{4,0},{5,1},{6,2},{7,3},{8,12},{9,13},{10,... | collective-permute-start | bytes 700424 | tf_op jit(solution)/shard_map/ppermute | solution.py:15
  360.7 7.7 %collective-permute-start.27 = (bf16[2,24,2432]{2,1,0:T(8,128)(2,1)S(1)}, bf16[2,24,2432]{2,1,0:T(8,128)(2,1)S(1)}, u32[]{:S(2)}, u32[]{:S(2)}) collective-permute-start(bf16[2,24,2432]{2,1,0:T(8,128)(2,1)S(1)} %get-tuple-element.87), channel_id=1, source_target_pairs={{0,2},{1,3},{2,0},{3,1},{4,6},{5,7},{6,4},{7,5},{8,10},{9,11},{10,... | collective-permute-start | bytes 700424 | tf_op jit(solution)/shard_map/ppermute | solution.py:15
  362.4 23.8 %collective-permute-start.32 = (bf16[4,4,24,3840]{3,2,0,1:T(8,128)(2,1)S(1)}, bf16[4,4,24,3840]{3,2,0,1:T(8,128)(2,1)S(1)}, u32[]{:S(2)}, u32[]{:S(2)}) collective-permute-start(bf16[4,4,24,3840]{3,2,0,1:T(8,128)(2,1)S(1)} %pad_maximum_fusion), channel_id=1, source_target_pairs={{0,1},{1,0},{2,3},{3,2},{4,5},{5,4},{6,7},{7,6},{8,9},{9,8},{10,11... | collective-permute-start | bytes 8847368 | tf_op jit(solution)/shard_map/ppermute | solution.py:15
  368.5 13.6 %collective-permute-start.26 = (bf16[4,24,2432]{2,1,0:T(8,128)(2,1)S(1)}, bf16[4,24,2432]{2,1,0:T(8,128)(2,1)S(1)}, u32[]{:S(2)}, u32[]{:S(2)}) collective-permute-start(bf16[4,24,2432]{2,1,0:T(8,128)(2,1)S(1)} %pad_maximum_fusion.6), channel_id=1, source_target_pairs={{0,2},{1,3},{2,0},{3,1},{4,6},{5,7},{6,4},{7,5},{8,10},{9,11},{10,... | collective-permute-start | bytes 1400840 | tf_op jit(solution)/shard_map/ppermute | solution.py:15
  370.1 13.6 %collective-permute-start.28 = (bf16[4,24,2432]{2,1,0:T(8,128)(2,1)S(1)}, bf16[4,24,2432]{2,1,0:T(8,128)(2,1)S(1)}, u32[]{:S(2)}, u32[]{:S(2)}) collective-permute-start(bf16[4,24,2432]{2,1,0:T(8,128)(2,1)S(1)} %pad_maximum_fusion.7), channel_id=1, source_target_pairs={{0,4},{1,5},{2,6},{3,7},{4,0},{5,1},{6,2},{7,3},{8,12},{9,13},{10,... | collective-permute-start | bytes 1400840 | tf_op jit(solution)/shard_map/ppermute | solution.py:15
  371.6 18.3 %collective-permute-start.41 = (bf16[2,96,768]{2,1,0:T(8,128)(2,1)S(1)}, bf16[2,96,768]{2,1,0:T(8,128)(2,1)S(1)}, u32[]{:S(2)}, u32[]{:S(2)}) collective-permute-start(bf16[2,96,768]{2,1,0:T(8,128)(2,1)S(1)} %get-tuple-element.79), channel_id=1, source_target_pairs={{0,4},{1,5},{2,6},{3,7},{4,0},{5,1},{6,2},{7,3},{8,12},{9,13},{10,... | collective-permute-start | bytes 884744 | tf_op jit(solution)/shard_map/ppermute | solution.py:15
  373.1 17.3 %collective-permute-start.43 = (bf16[2,96,768]{2,1,0:T(8,128)(2,1)S(1)}, bf16[2,96,768]{2,1,0:T(8,128)(2,1)S(1)}, u32[]{:S(2)}, u32[]{:S(2)}) collective-permute-start(bf16[2,96,768]{2,1,0:T(8,128)(2,1)S(1)} %get-tuple-element.81), channel_id=1, source_target_pairs={{0,2},{1,3},{2,0},{3,1},{4,6},{5,7},{6,4},{7,5},{8,10},{9,11},{10,... | collective-permute-start | bytes 884744 | tf_op jit(solution)/shard_map/ppermute | solution.py:15
  384.0 20.9 %collective-permute-start.29 = (bf16[1,24,2432]{2,1,0:T(8,128)(2,1)S(1)}, bf16[1,24,2432]{2,1,0:T(8,128)(2,1)S(1)}, u32[]{:S(2)}, u32[]{:S(2)}) collective-permute-start(bf16[1,24,2432]{2,1,0:T(8,128)(2,1)S(1)} %get-tuple-element.99), channel_id=1, source_target_pairs={{0,8},{1,9},{2,10},{3,11},{4,12},{5,13},{6,14},{7,15},{8,16},{9,17... | collective-permute-start | bytes 350216 | tf_op jit(solution)/shard_map/ppermute | solution.py:15
  384.6 20.8 %collective-permute-start.30 = (bf16[1,24,2432]{2,1,0:T(8,128)(2,1)S(1)}, bf16[1,24,2432]{2,1,0:T(8,128)(2,1)S(1)}, u32[]{:S(2)}, u32[]{:S(2)}) collective-permute-start(bf16[1,24,2432]{2,1,0:T(8,128)(2,1)S(1)} %get-tuple-element.101), channel_id=1, source_target_pairs={{0,16},{1,17},{2,18},{3,19},{4,20},{5,21},{6,22},{7,23},{8,24},{9,... | collective-permute-start | bytes 350216 | tf_op jit(solution)/shard_map/ppermute | solution.py:15
  386.1 19.3 %collective-permute-start.31 = (bf16[1,24,2432]{2,1,0:T(8,128)(2,1)S(1)}, bf16[1,24,2432]{2,1,0:T(8,128)(2,1)S(1)}, u32[]{:S(2)}, u32[]{:S(2)}) collective-permute-start(bf16[1,24,2432]{2,1,0:T(8,128)(2,1)S(1)} %get-tuple-element.100), channel_id=1, source_target_pairs={{0,24},{1,25},{2,26},{3,27},{4,28},{5,29},{6,30},{7,31},{8,0},{9,1... | collective-permute-start | bytes 350216 | tf_op jit(solution)/shard_map/ppermute | solution.py:15
  389.9 9.3 %collective-permute-start.33 = (bf16[2,24,3840]{2,1,0:T(8,128)(2,1)S(1)}, bf16[2,24,3840]{2,1,0:T(8,128)(2,1)S(1)}, u32[]{:S(2)}, u32[]{:S(2)}) collective-permute-start(bf16[2,24,3840]{2,1,0:T(8,128)(2,1)S(1)} %get-tuple-element.73), channel_id=1, source_target_pairs={{0,4},{1,5},{2,6},{3,7},{4,0},{5,1},{6,2},{7,3},{8,12},{9,13},{10,... | collective-permute-start | bytes 1105928 | tf_op jit(solution)/shard_map/ppermute | solution.py:15
  390.5 9.9 %collective-permute-start.35 = (bf16[2,24,3840]{2,1,0:T(8,128)(2,1)S(1)}, bf16[2,24,3840]{2,1,0:T(8,128)(2,1)S(1)}, u32[]{:S(2)}, u32[]{:S(2)}) collective-permute-start(bf16[2,24,3840]{2,1,0:T(8,128)(2,1)S(1)} %get-tuple-element.75), channel_id=1, source_target_pairs={{0,2},{1,3},{2,0},{3,1},{4,6},{5,7},{6,4},{7,5},{8,10},{9,11},{10,... | collective-permute-start | bytes 1105928 | tf_op jit(solution)/shard_map/ppermute | solution.py:15
  399.1 16.5 %collective-permute-start.42 = (bf16[4,96,768]{2,1,0:T(8,128)(2,1)}, bf16[4,96,768]{2,1,0:T(8,128)(2,1)}, u32[]{:S(2)}, u32[]{:S(2)}) collective-permute-start(bf16[4,96,768]{2,1,0:T(8,128)(2,1)} %pad_maximum_fusion.4), channel_id=1, source_target_pairs={{0,2},{1,3},{2,0},{3,1},{4,6},{5,7},{6,4},{7,5},{8,10},{9,11},{10,... | collective-permute-start | bytes 1769480 | tf_op jit(solution)/shard_map/ppermute | solution.py:15
  400.4 16.9 %collective-permute-start.44 = (bf16[4,96,768]{2,1,0:T(8,128)(2,1)}, bf16[4,96,768]{2,1,0:T(8,128)(2,1)}, u32[]{:S(2)}, u32[]{:S(2)}) collective-permute-start(bf16[4,96,768]{2,1,0:T(8,128)(2,1)} %pad_maximum_fusion.5), channel_id=1, source_target_pairs={{0,4},{1,5},{2,6},{3,7},{4,0},{5,1},{6,2},{7,3},{8,12},{9,13},{10,... | collective-permute-start | bytes 1769480 | tf_op jit(solution)/shard_map/ppermute | solution.py:15
  404.9 21.6 %collective-permute-start.34 = (bf16[4,24,3840]{2,1,0:T(8,128)(2,1)}, bf16[4,24,3840]{2,1,0:T(8,128)(2,1)}, u32[]{:S(2)}, u32[]{:S(2)}) collective-permute-start(bf16[4,24,3840]{2,1,0:T(8,128)(2,1)} %pad_maximum_fusion.2), channel_id=1, source_target_pairs={{0,2},{1,3},{2,0},{3,1},{4,6},{5,7},{6,4},{7,5},{8,10},{9,11},{10,... | collective-permute-start | bytes 2211848 | tf_op jit(solution)/shard_map/ppermute | solution.py:15
  405.4 21.1 %collective-permute-start.36 = (bf16[4,24,3840]{2,1,0:T(8,128)(2,1)}, bf16[4,24,3840]{2,1,0:T(8,128)(2,1)}, u32[]{:S(2)}, u32[]{:S(2)}) collective-permute-start(bf16[4,24,3840]{2,1,0:T(8,128)(2,1)} %pad_maximum_fusion.3), channel_id=1, source_target_pairs={{0,4},{1,5},{2,6},{3,7},{4,0},{5,1},{6,2},{7,3},{8,12},{9,13},{10,... | collective-permute-start | bytes 2211848 | tf_op jit(solution)/shard_map/ppermute | solution.py:15
  419.0 10.3 %collective-permute-start.45 = (bf16[1,96,768]{2,1,0:T(8,128)(2,1)S(1)}, bf16[1,96,768]{2,1,0:T(8,128)(2,1)S(1)}, u32[]{:S(2)}, u32[]{:S(2)}) collective-permute-start(bf16[1,96,768]{2,1,0:T(8,128)(2,1)S(1)} %get-tuple-element.96), channel_id=1, source_target_pairs={{0,8},{1,9},{2,10},{3,11},{4,12},{5,13},{6,14},{7,15},{8,16},{9,17... | collective-permute-start | bytes 442376 | tf_op jit(solution)/shard_map/ppermute | solution.py:15
  419.1 13.1 %collective-permute-start.46 = (bf16[1,96,768]{2,1,0:T(8,128)(2,1)S(1)}, bf16[1,96,768]{2,1,0:T(8,128)(2,1)S(1)}, u32[]{:S(2)}, u32[]{:S(2)}) collective-permute-start(bf16[1,96,768]{2,1,0:T(8,128)(2,1)S(1)} %get-tuple-element.98), channel_id=1, source_target_pairs={{0,16},{1,17},{2,18},{3,19},{4,20},{5,21},{6,22},{7,23},{8,24},{9,... | collective-permute-start | bytes 442376 | tf_op jit(solution)/shard_map/ppermute | solution.py:15
  419.1 13.0 %collective-permute-start.47 = (bf16[1,96,768]{2,1,0:T(8,128)(2,1)S(1)}, bf16[1,96,768]{2,1,0:T(8,128)(2,1)S(1)}, u32[]{:S(2)}, u32[]{:S(2)}) collective-permute-start(bf16[1,96,768]{2,1,0:T(8,128)(2,1)S(1)} %get-tuple-element.97), channel_id=1, source_target_pairs={{0,24},{1,25},{2,26},{3,27},{4,28},{5,29},{6,30},{7,31},{8,0},{9,1... | collective-permute-start | bytes 442376 | tf_op jit(solution)/shard_map/ppermute | solution.py:15
  428.2 9.0 %collective-permute-start.37 = (bf16[1,24,3840]{2,1,0:T(8,128)(2,1)S(1)}, bf16[1,24,3840]{2,1,0:T(8,128)(2,1)S(1)}, u32[]{:S(2)}, u32[]{:S(2)}) collective-permute-start(bf16[1,24,3840]{2,1,0:T(8,128)(2,1)S(1)} %get-tuple-element.93), channel_id=1, source_target_pairs={{0,8},{1,9},{2,10},{3,11},{4,12},{5,13},{6,14},{7,15},{8,16},{9,17... | collective-permute-start | bytes 552968 | tf_op jit(solution)/shard_map/ppermute | solution.py:15
  428.3 15.5 %collective-permute-start.38 = (bf16[1,24,3840]{2,1,0:T(8,128)(2,1)S(1)}, bf16[1,24,3840]{2,1,0:T(8,128)(2,1)S(1)}, u32[]{:S(2)}, u32[]{:S(2)}) collective-permute-start(bf16[1,24,3840]{2,1,0:T(8,128)(2,1)S(1)} %get-tuple-element.95), channel_id=1, source_target_pairs={{0,16},{1,17},{2,18},{3,19},{4,20},{5,21},{6,22},{7,23},{8,24},{9,... | collective-permute-start | bytes 552968 | tf_op jit(solution)/shard_map/ppermute | solution.py:15
  429.3 14.5 %collective-permute-start.39 = (bf16[1,24,3840]{2,1,0:T(8,128)(2,1)S(1)}, bf16[1,24,3840]{2,1,0:T(8,128)(2,1)S(1)}, u32[]{:S(2)}, u32[]{:S(2)}) collective-permute-start(bf16[1,24,3840]{2,1,0:T(8,128)(2,1)S(1)} %get-tuple-element.94), channel_id=1, source_target_pairs={{0,24},{1,25},{2,26},{3,27},{4,28},{5,29},{6,30},{7,31},{8,0},{9,1... | collective-permute-start | bytes 552968 | tf_op jit(solution)/shard_map/ppermute | solution.py:15
  (68 other events, 845.7 us)
